TPU v7x, 32 devices: a whole 2x2x4 slice. The times are simulated.
32 devices in a mesh: items: 8 (over z, y), rows: 4 (over x, core).
Axes of the slice: x: 2, y: 2, z: 4, core: 2. Of those that a mesh axis runs over, the one named last changes fastest.
Arguments:
- images: bfloat16 [128, 3, 256, 256], P('items', None, 'rows'), may hold values from -6 to 6
- item_segment: int32 [128], P('items'), may hold values from 0 to 3, as said below
- conv_weight: bfloat16 [32, 3, 3, 3], replicated, may hold values from -1.25 to 1.25
- conv_bias: bfloat16 [32], replicated, may hold values from -1.5 to 1.5
- patch_weight: bfloat16 [8192, 768], replicated, may hold values from -0.125 to 0.125
- patch_bias: bfloat16 [768], replicated, may hold values from -1.5 to 1.5
- norm1_gain: bfloat16 [768], replicated, may hold values from 0.3984375 to 1.59375
- norm1_bias: bfloat16 [768], replicated, may hold values from -1.5 to 1.5
- query_weight: bfloat16 [768, 768], replicated, may hold values from -0.21875 to 0.21875
- query_bias: bfloat16 [768], replicated, may hold values from -1.5 to 1.5
- key_weight: bfloat16 [768, 768], replicated, may hold values from -0.21875 to 0.21875
- value_weight: bfloat16 [768, 768], replicated, may hold values from -0.21875 to 0.21875
- value_bias: bfloat16 [768], replicated, may hold values from -1.5 to 1.5
- output_weight: bfloat16 [768, 768], replicated, may hold values from -1.75 to 1.75
- output_bias: bfloat16 [768], replicated, may hold values from -1.5 to 1.5
- norm2_gain: bfloat16 [768], replicated, may hold values from 0.3984375 to 1.59375
- norm2_bias: bfloat16 [768], replicated, may hold values from -1.5 to 1.5
- hidden_weight: bfloat16 [768, 3072], replicated, may hold values from -0.21875 to 0.21875
- hidden_bias: bfloat16 [3072], replicated, may hold values from -1.5 to 1.5
- result_weight: bfloat16 [3072, 768], replicated, may hold values from -0.15625 to 0.15625
- result_bias: bfloat16 [768], replicated, may hold values from -1.5 to 1.5
- cotangent: bfloat16 [32768, 768], P(('items', 'rows')), may hold values from -6 to 6
Outputs:
- block_out: bfloat16 [32768, 768], P(('items', 'rows'))
- image_grad: float32 [128, 3, 256, 256], P('items', None, 'rows')
- conv_weight_grad: float32 [32, 3, 3, 3], replicated
- conv_bias_grad: float32 [32], replicated
- patch_weight_grad: float32 [8192, 768], P('items', 'rows')
- patch_bias_grad: float32 [768], replicated
- norm1_gain_grad: float32 [768], replicated
- norm1_bias_grad: float32 [768], replicated
- query_weight_grad: float32 [768, 768], P('items', 'rows')
- query_bias_grad: float32 [768], replicated
- key_weight_grad: float32 [768, 768], P('items', 'rows')
- value_weight_grad: float32 [768, 768], P('items', 'rows')
- value_bias_grad: float32 [768], replicated
- output_weight_grad: float32 [768, 768], P('items', 'rows')
- output_bias_grad: float32 [768], replicated
- norm2_gain_grad: float32 [768], replicated
- norm2_bias_grad: float32 [768], replicated
- hidden_weight_grad: float32 [768, 3072], P('items', 'rows')
- hidden_bias_grad: float32 [3072], replicated
- result_weight_grad: float32 [3072, 768], P('items', 'rows')
- result_bias_grad: float32 [768], replicated
Inputs may be any that keep to these rules, and one draw needn't show every extreme that they name: `item_segment`: within each sequence of 4 consecutive items the ids start at 0 and rise by 0 or 1 from one item to the next.
All inputs are finite; a program needn't handle non-finite values.
Results may differ from a plain program's by a relative error of at most 0.02.
Values may be sent and summed in bfloat16 or wider, within the bound.
A program may use at most 640 MiB of HBM per device.

v0:
```python
import jax
import jax.numpy as jnp
from jax import lax
from jax.sharding import PartitionSpec as P

D = 768
HEADS = 12
HD = 64
IMG = 256
PATCH = 16
SEQ_ITEMS = 4
SEQ_DEV = 1
NPATCH = 256
TOK = 1024


def padded_2(cells, sides, width):
    for axis, dim in sides:
        count = lax.axis_size(axis)
        ends = count - 1
        head = lax.slice_in_dim(cells, 0, width, axis=dim)
        tail = lax.slice_in_dim(cells, cells.shape[dim] - width, cells.shape[dim], axis=dim)
        cells = jnp.concatenate(
            [
                lax.ppermute(tail, axis, [(i, (i + 1) % count) for i in range(ends)]),
                cells,
                lax.ppermute(head, axis, [((i + 1) % count, i) for i in range(ends)]),
            ],
            axis=dim,
        )
    return cells


def layer_norm(values, scaling, shifting):
    centred = values - jnp.mean(values, axis=-1, keepdims=True)
    spread = jnp.mean(centred * centred, axis=-1, keepdims=True)
    return centred * lax.rsqrt(spread + 1e-06) * scaling + shifting


def gelu_grad(pre_act, upstream):
    _, pullback = jax.vjp(jax.nn.gelu, pre_act)
    return pullback(upstream)[0]


def stack_taps(padded):
    height = padded.shape[2] - 2
    width = padded.shape[3]
    widened = jnp.pad(padded, ((0, 0), (0, 0), (0, 0), (1, 1)))
    shifted = [
        widened[:, :, row_tap : row_tap + height, col_tap : col_tap + width]
        for row_tap in range(3)
        for col_tap in range(3)
    ]
    stacked = jnp.stack(shifted, axis=2)
    return stacked.reshape(padded.shape[0], padded.shape[1] * 9, height, width)


def convolve(stacked, kernel):
    flat_kernel = kernel.reshape(kernel.shape[0], -1)
    return jnp.einsum("nkhw,ok->nohw", stacked, flat_kernel, preferred_element_type=jnp.float32)


def convolve_back(grad_padded, kernel):
    height = grad_padded.shape[2] - 2
    width = grad_padded.shape[3]
    widened = jnp.pad(grad_padded, ((0, 0), (0, 0), (0, 0), (1, 1)))
    total = jnp.zeros((grad_padded.shape[0], kernel.shape[1], height, width), jnp.float32)
    for row_tap in range(3):
        for col_tap in range(3):
            window = widened[
                :, :, 2 - row_tap : 2 - row_tap + height, 2 - col_tap : 2 - col_tap + width
            ]
            total = total + jnp.einsum(
                "nohw,oc->nchw",
                window,
                kernel[:, :, row_tap, col_tap],
                preferred_element_type=jnp.float32,
            )
    return total


def matmul(left, right):
    return jnp.dot(left, right, preferred_element_type=jnp.float32)


def inner_left(left, right):
    return jnp.einsum("tf,td->fd", left, right, preferred_element_type=jnp.float32)


def inner_right(left, right):
    return jnp.einsum("td,fd->tf", left, right, preferred_element_type=jnp.float32)


def column_sums(values):
    return jnp.sum(values.astype(jnp.float32), axis=0)


def to_patches(activated):
    count, chans, height, width = activated.shape
    tiles = activated.reshape(count, chans, height // PATCH, PATCH, width // PATCH, PATCH)
    return tiles.transpose(0, 2, 4, 1, 3, 5).reshape(
        count * (height // PATCH) * (width // PATCH), chans * PATCH * PATCH
    )


def from_patches(flat, count, chans, height, width):
    tiles = flat.reshape(count, height // PATCH, width // PATCH, chans, PATCH, PATCH)
    return tiles.transpose(0, 3, 1, 4, 2, 5).reshape(count, chans, height, width)


def item_mask(segments):
    order = jnp.arange(SEQ_ITEMS, dtype=jnp.int32)
    same = segments[:, :, None] == segments[:, None, :]
    first = jnp.min(jnp.where(same, order[None, None, :], SEQ_ITEMS), axis=2)
    group = order[None, :] - first
    allowed = same & (group[:, None, :] <= group[:, :, None])
    return jnp.repeat(jnp.repeat(allowed, NPATCH, axis=1), NPATCH, axis=2)


def masked_scores(query_part, key_heads, allowed_part, score_scale):
    scores = (
        jnp.einsum("sqhd,skhd->shqk", query_part, key_heads, preferred_element_type=jnp.float32)
        * score_scale
    )
    return jnp.where(allowed_part[:, None], scores, -1e30)


def on_device(
    images,
    item_segment,
    conv_weight,
    conv_bias,
    patch_weight,
    patch_bias,
    norm1_gain,
    norm1_bias,
    query_weight,
    query_bias,
    key_weight,
    value_weight,
    value_bias,
    output_weight,
    output_bias,
    norm2_gain,
    norm2_bias,
    hidden_weight,
    hidden_bias,
    result_weight,
    result_bias,
    cotangent,
):
    item_count = SEQ_DEV * SEQ_ITEMS
    first_item = lax.axis_index("rows") * item_count
    segments = lax.dynamic_slice_in_dim(item_segment, first_item, item_count).reshape(
        SEQ_DEV, SEQ_ITEMS
    )
    allowed = item_mask(segments)
    padded = padded_2(images, (("rows", 2),), 1)
    stacked = stack_taps(padded)
    pre_act = convolve(stacked, conv_weight) + conv_bias.astype(jnp.float32)[None, :, None, None]
    activated = jax.nn.gelu(pre_act).astype(jnp.bfloat16)
    stem_count, chans, height, width = activated.shape
    patches = to_patches(activated)
    embedded = (matmul(patches, patch_weight) + patch_bias.astype(jnp.float32)).astype(jnp.bfloat16)
    tokens = lax.all_to_all(
        embedded.reshape(stem_count, -1, IMG // PATCH, D),
        "rows",
        split_axis=0,
        concat_axis=1,
        tiled=True,
    ).reshape(-1, D)
    stream = tokens.astype(jnp.float32)
    gain_one = norm1_gain.astype(jnp.float32)
    shift_one = norm1_bias.astype(jnp.float32)
    gain_two = norm2_gain.astype(jnp.float32)
    shift_two = norm2_bias.astype(jnp.float32)
    normed1 = layer_norm(stream, gain_one, shift_one).astype(jnp.bfloat16)
    queries = (matmul(normed1, query_weight) + query_bias.astype(jnp.float32)).astype(jnp.bfloat16)
    keys_all = matmul(normed1, key_weight).astype(jnp.bfloat16)
    values_all = (matmul(normed1, value_weight) + value_bias.astype(jnp.float32)).astype(
        jnp.bfloat16
    )
    head_shape = (SEQ_DEV, TOK, HEADS, HD)
    query_heads = queries.reshape(head_shape)
    key_heads = keys_all.reshape(head_shape)
    value_heads = values_all.reshape(head_shape)
    score_scale = HD ** (-0.5)
    block_rows = min(512, TOK)
    outputs = []
    kept_stats = []
    for offset in range(0, TOK, block_rows):
        query_part = query_heads[:, offset : offset + block_rows]
        scores = masked_scores(
            query_part, key_heads, allowed[:, offset : offset + block_rows], score_scale
        )
        row_max = jnp.max(scores, axis=-1, keepdims=True)
        raised = jnp.exp(scores - row_max)
        row_total = jnp.sum(raised, axis=-1, keepdims=True)
        probs_low = (raised / row_total).astype(jnp.bfloat16)
        outputs.append(
            jnp.einsum(
                "shqk,skhd->sqhd", probs_low, value_heads, preferred_element_type=jnp.float32
            ).astype(jnp.bfloat16)
        )
        kept_stats.append((row_max, row_total))
    attended = jnp.concatenate(outputs, axis=1).reshape(-1, D)
    middle = stream + matmul(attended, output_weight) + output_bias.astype(jnp.float32)
    normed2 = layer_norm(middle, gain_two, shift_two).astype(jnp.bfloat16)
    hidden_pre = matmul(normed2, hidden_weight) + hidden_bias.astype(jnp.float32)
    hidden_act = jax.nn.gelu(hidden_pre).astype(jnp.bfloat16)
    block_out = (
        middle + matmul(hidden_act, result_weight) + result_bias.astype(jnp.float32)
    ).astype(jnp.bfloat16)
    upstream = cotangent.astype(jnp.float32)
    result_weight_grad = inner_left(hidden_act, cotangent)
    result_bias_grad = column_sums(cotangent)
    hidden_grad = gelu_grad(hidden_pre, inner_right(cotangent, result_weight)).astype(jnp.bfloat16)
    hidden_weight_grad = inner_left(normed2, hidden_grad)
    hidden_bias_grad = column_sums(hidden_grad)
    _, norm_pull_two = jax.vjp(layer_norm, middle, gain_two, shift_two)
    middle_extra, norm2_gain_grad, norm2_bias_grad = norm_pull_two(
        inner_right(hidden_grad, hidden_weight)
    )
    middle_grad = upstream + middle_extra
    branch_grad = middle_grad.astype(jnp.bfloat16)
    output_weight_grad = inner_left(attended, branch_grad)
    output_bias_grad = column_sums(branch_grad)
    attended_grad = inner_right(branch_grad, output_weight).astype(jnp.bfloat16).reshape(head_shape)
    key_accum = jnp.zeros(head_shape, jnp.float32)
    value_accum = jnp.zeros(head_shape, jnp.float32)
    query_parts = []
    for offset in range(0, TOK, block_rows):
        query_part = query_heads[:, offset : offset + block_rows]
        row_max, row_total = kept_stats[offset // block_rows]
        scores = masked_scores(
            query_part, key_heads, allowed[:, offset : offset + block_rows], score_scale
        )
        probs = jnp.exp(scores - row_max) / row_total
        probs_low = probs.astype(jnp.bfloat16)
        grad_part = attended_grad[:, offset : offset + block_rows]
        prob_grad = jnp.einsum(
            "sqhd,skhd->shqk", grad_part, value_heads, preferred_element_type=jnp.float32
        )
        score_grad = (
            probs * (prob_grad - jnp.sum(probs * prob_grad, axis=-1, keepdims=True)) * score_scale
        ).astype(jnp.bfloat16)
        query_parts.append(
            jnp.einsum(
                "shqk,skhd->sqhd", score_grad, key_heads, preferred_element_type=jnp.float32
            ).astype(jnp.bfloat16)
        )
        key_accum = key_accum + jnp.einsum(
            "shqk,sqhd->skhd", score_grad, query_part, preferred_element_type=jnp.float32
        )
        value_accum = value_accum + jnp.einsum(
            "shqk,sqhd->skhd", probs_low, grad_part, preferred_element_type=jnp.float32
        )
    query_grad = jnp.concatenate(query_parts, axis=1).reshape(-1, D)
    key_grad = key_accum.astype(jnp.bfloat16).reshape(-1, D)
    value_grad = value_accum.astype(jnp.bfloat16).reshape(-1, D)
    query_weight_grad = inner_left(normed1, query_grad)
    query_bias_grad = column_sums(query_grad)
    key_weight_grad = inner_left(normed1, key_grad)
    value_weight_grad = inner_left(normed1, value_grad)
    value_bias_grad = column_sums(value_grad)
    normed1_grad = (
        inner_right(query_grad, query_weight)
        + inner_right(key_grad, key_weight)
        + inner_right(value_grad, value_weight)
    )
    _, norm_pull_one = jax.vjp(layer_norm, stream, gain_one, shift_one)
    stream_extra, norm1_gain_grad, norm1_bias_grad = norm_pull_one(normed1_grad)
    token_grad = (middle_grad + stream_extra).astype(jnp.bfloat16)
    embed_grad = lax.all_to_all(
        token_grad.reshape(SEQ_DEV * SEQ_ITEMS, IMG // PATCH, IMG // PATCH, D),
        "rows",
        split_axis=1,
        concat_axis=0,
        tiled=True,
    ).reshape(-1, D)
    patch_weight_grad = inner_left(patches, embed_grad)
    patch_bias_grad = column_sums(embed_grad)
    activated_grad = from_patches(
        inner_right(embed_grad, patch_weight), stem_count, chans, height, width
    )
    pre_grad = gelu_grad(pre_act, activated_grad).astype(jnp.bfloat16)
    conv_bias_grad = jnp.sum(pre_grad.astype(jnp.float32), axis=(0, 2, 3))
    conv_weight_grad = jnp.einsum(
        "nohw,nkhw->ok", pre_grad, stacked, preferred_element_type=jnp.float32
    ).reshape(conv_weight.shape)
    grad_padded = padded_2(pre_grad, (("rows", 2),), 1)
    image_grad = convolve_back(grad_padded, conv_weight)
    small = lax.psum(
        (
            conv_weight_grad,
            conv_bias_grad,
            patch_bias_grad,
            norm1_gain_grad,
            norm1_bias_grad,
            query_bias_grad,
            value_bias_grad,
            output_bias_grad,
            norm2_gain_grad,
            norm2_bias_grad,
            hidden_bias_grad,
            result_bias_grad,
        ),
        ("items", "rows"),
    )
    section = (
        lax.psum_scatter(
            patch_weight_grad.astype(jnp.bfloat16), "items", scatter_dimension=0, tiled=True
        ).astype(jnp.float32),
        lax.psum_scatter(
            query_weight_grad.astype(jnp.bfloat16), "items", scatter_dimension=0, tiled=True
        ).astype(jnp.float32),
        lax.psum_scatter(
            key_weight_grad.astype(jnp.bfloat16), "items", scatter_dimension=0, tiled=True
        ).astype(jnp.float32),
        lax.psum_scatter(
            value_weight_grad.astype(jnp.bfloat16), "items", scatter_dimension=0, tiled=True
        ).astype(jnp.float32),
        lax.psum_scatter(
            output_weight_grad.astype(jnp.bfloat16), "items", scatter_dimension=0, tiled=True
        ).astype(jnp.float32),
        lax.psum_scatter(
            hidden_weight_grad.astype(jnp.bfloat16), "items", scatter_dimension=0, tiled=True
        ).astype(jnp.float32),
        lax.psum_scatter(
            result_weight_grad.astype(jnp.bfloat16), "items", scatter_dimension=0, tiled=True
        ).astype(jnp.float32),
    )
    summed = (
        lax.psum_scatter(
            section[0].astype(jnp.bfloat16), "rows", scatter_dimension=1, tiled=True
        ).astype(jnp.float32),
        lax.psum_scatter(
            section[1].astype(jnp.bfloat16), "rows", scatter_dimension=1, tiled=True
        ).astype(jnp.float32),
        lax.psum_scatter(
            section[2].astype(jnp.bfloat16), "rows", scatter_dimension=1, tiled=True
        ).astype(jnp.float32),
        lax.psum_scatter(
            section[3].astype(jnp.bfloat16), "rows", scatter_dimension=1, tiled=True
        ).astype(jnp.float32),
        lax.psum_scatter(
            section[4].astype(jnp.bfloat16), "rows", scatter_dimension=1, tiled=True
        ).astype(jnp.float32),
        lax.psum_scatter(
            section[5].astype(jnp.bfloat16), "rows", scatter_dimension=1, tiled=True
        ).astype(jnp.float32),
        lax.psum_scatter(
            section[6].astype(jnp.bfloat16), "rows", scatter_dimension=1, tiled=True
        ).astype(jnp.float32),
    )
    return (
        block_out,
        image_grad,
        small[0],
        small[1],
        summed[0],
        small[2],
        small[3],
        small[4],
        summed[1],
        small[5],
        summed[2],
        summed[3],
        small[6],
        summed[4],
        small[7],
        small[8],
        small[9],
        summed[5],
        small[10],
        summed[6],
        small[11],
    )


def solution(mesh):
    placed = (
        P("items", None, "rows", None),
        P("items"),
        P(),
        P(),
        P(),
        P(),
        P(),
        P(),
        P(),
        P(),
        P(),
        P(),
        P(),
        P(),
        P(),
        P(),
        P(),
        P(),
        P(),
        P(),
        P(),
        P(("items", "rows"), None),
    )
    return jax.shard_map(
        on_device,
        mesh=mesh,
        in_specs=placed,
        out_specs=(
            P(("items", "rows"), None),
            P("items", None, "rows", None),
            P(),
            P(),
            P("items", "rows"),
            P(),
            P(),
            P(),
            P("items", "rows"),
            P(),
            P("items", "rows"),
            P("items", "rows"),
            P(),
            P("items", "rows"),
            P(),
            P(),
            P(),
            P("items", "rows"),
            P(),
            P("items", "rows"),
            P(),
        ),
        check_vma=False,
    )
```

profile of v0, /device:TPU:0, one launch (start us, length us, event | category | flops | bytes accessed | tf_op | source)
XLA Modules:
  0.0 1613.1 jit_solution(13263117179323279298)
XLA Ops:
  27.2 25.8 %fusion.14 = (bf16[16,32,64,256]{3,1,2,0:T(8,128)(2,1)}, f32[16,64,256,32]{2,3,1,0:T(8,128)}) fusion(f32[32]{0:T(128)S(1)} %convert_element_type.266, bf16[32,27]{0,1:T(8,128)(2,1)S(1)} %reshape.525, bf16[16,27,64,256]{3,2,1,0:T(8,128)(2,1)S(1)} %bitcast.327), kind=kOutput, calls=%fused_computation.21 | convolution fusion | flops 536870912 | bytes 64489280 | tf_op jit(solution)/shard_map/nkhw,ok->nohw/dot_general | solution.py:60
  53.0 54.0 %copy.104 = bf16[16,32,64,256]{1,3,2,0:T(8,128)(2,1)} copy(bf16[16,32,64,256]{3,1,2,0:T(8,128)(2,1)} %get-tuple-element.150) | data formatting | bytes 33554432 | tf_op jit(solution)/shard_map/convert_element_type | solution.py:161
  107.0 142.9 %copy.105 = bf16[16,4,16,32,16,16]{5,4,3,2,1,0:T(8,128)(2,1)} copy(bf16[16,4,16,32,16,16]{3,5,2,4,1,0:T(8,128)(2,1)} %bitcast.18) | data formatting | bytes 33554432 | tf_op jit(solution)/shard_map/transpose | solution.py:101
  249.9 224.9 %reshape.527 = bf16[1024,8192]{1,0:T(8,128)(2,1)} reshape(bf16[16,4,16,32,16,16]{5,4,3,2,1,0:T(8,128)(2,1)} %copy.105) | data formatting | bytes 33554432 | tf_op jit(solution)/shard_map/reshape | solution.py:101
  474.9 19.9 %add_convert_fusion.9 = bf16[1024,768]{1,0:T(8,128)(2,1)} fusion(bf16[1024,8192]{1,0:T(8,128)(2,1)} %reshape.527, bf16[8192,768]{1,0:T(8,128)(2,1)} %param.26, f32[768]{0:T(1024)S(1)} %copy-done.74), kind=kOutput, calls=%fused_computation.133 | convolution fusion | flops 12886474752 | bytes 30936064 | tf_op jit(solution)/shard_map/dot_general | solution.py:83
  494.8 4.9 all-to-all-start
  501.9 4.5 broadcast_in_dim.103
  512.6 7.1 all-to-all-done
  529.3 10.1 fusion.139
  539.4 10.1 fusion.138
  550.9 33.8 %fusion.170 = (f32[12,512]{1,0:T(8,128)S(1)}, f32[12,512,1024]{2,1,0:T(8,128)}) fusion(f32[12,512,1024]{2,1,0:T(8,128)} %fusion.139, pred[512,1024]{1,0:T(8,128)(4,1)} %get-tuple-element.138), kind=kOutput, calls=%fused_computation.230 | output fusion | flops 37749760 | bytes 50880512 | tf_op jit(solution)/shard_map/sub | solution.py:197
  584.8 33.2 %fusion.171 = (f32[12,512]{1,0:T(8,128)S(1)}, f32[12,512,1024]{2,1,0:T(8,128)}) fusion(f32[12,512,1024]{2,1,0:T(8,128)} %fusion.138, pred[512,1024]{1,0:T(8,128)(4,1)S(1)} %get-tuple-element.137), kind=kOutput, calls=%fused_computation.231 | output fusion | flops 37749760 | bytes 50880512 | tf_op jit(solution)/shard_map/sub | solution.py:197
  618.0 10.3 fusion.127
  628.3 10.6 fusion.130
  641.6 11.1 fusion.162
  652.7 17.0 %convert_reduce_fusion.1 = (f32[3072]{0:T(1024)}, bf16[1024,3072]{1,0:T(8,128)(2,1)}) fusion(f32[1024,3072]{1,0:T(8,128)} %fusion.162, f32[3072]{0:T(1024)S(1)} %copy-done.58, bf16[1024,768]{1,0:T(8,128)(2,1)S(1)} %copy-done.15, bf16[3072,768]{1,0:T(8,128)(2,1)S(1)} %bitcast.338), kind=kOutput, calls=%fused_computation.76 | convolution fusion | flops 4904186880 | bytes 25190400 | tf_op jit(solution)/shard_map/td,fd->tf/dot_general | solution.py:91
  669.7 8.5 multiply_reduce_fusion.2
  690.0 10.1 fusion.79
  700.8 11.2 convert_reduce_fusion.4
  715.7 13.6 fusion.141
  729.4 49.6 %fusion.124 = bf16[1,512,12,64]{1,3,2,0:T(8,128)(2,1)S(1)} fusion(bf16[1024,12,64]{0,2,1:T(8,128)(2,1)S(1)} %bitcast.290, f32[12,512,1024]{2,1,0:T(8,128)} %fusion.141, f32[12,512,1024]{2,1,0:T(8,128)} %get-tuple-element.153, f32[12,512]{1,0:T(8,128)} %copy-done.91), kind=kOutput, calls=%fused_computation.174 | convolution fusion | flops 849746944 | bytes 52715520 | tf_op jit(solution)/shard_map/shqk,skhd->sqhd/dot_general | solution.py:248
  779.0 13.5 fusion.140
  792.5 55.3 %fusion.121 = bf16[1,512,12,64]{1,3,2,0:T(8,128)(2,1)} fusion(bf16[1024,12,64]{0,2,1:T(8,128)(2,1)S(1)} %bitcast.291, f32[12,512,1024]{2,1,0:T(8,128)} %fusion.140, f32[12,512,1024]{2,1,0:T(8,128)} %get-tuple-element.155, f32[12,512]{1,0:T(8,128)} %copy-done.92), kind=kOutput, calls=%fused_computation.173 | convolution fusion | flops 849746944 | bytes 52715520 | tf_op jit(solution)/shard_map/shqk,skhd->sqhd/dot_general | solution.py:248
  854.4 51.5 %fusion.66 = f32[12,64,1024]{2,1,0:T(8,128)} fusion(f32[12,512,1024]{2,1,0:T(8,128)} %fusion.140, bf16[1,1024,12,64]{1,3,2,0:T(8,128)(2,1)S(1)} %bitcast.302, f32[12,512,1024]{2,1,0:T(8,128)} %get-tuple-element.155, f32[12,512]{1,0:T(8,128)} %copy-done.92), kind=kOutput, calls=%fused_computation.86 | convolution fusion | flops 849353728 | bytes 104660992 | tf_op jit(solution)/shard_map/shqk,sqhd->skhd/dot_general | solution.py:252
  905.9 51.6 %add_convert_fusion.3 = bf16[12,64,1024]{2,1,0:T(8,128)(2,1)} fusion(f32[12,64,1024]{2,1,0:T(8,128)} %fusion.66, f32[12,512,1024]{2,1,0:T(8,128)} %fusion.141, bf16[1,1024,12,64]{1,3,2,0:T(8,128)(2,1)S(1)} %bitcast.303, f32[12,512,1024]{2,1,0:T(8,128)} %get-tuple-element.153, f32[12,512]{1,0:T(8,128)} %copy-done.91), kind=kOutput, calls=%fused_computation.124 | convolution fusion | flops 850926592 | bytes 106233856 | tf_op jit(solution)/shard_map/shqk,sqhd->skhd/dot_general | solution.py:252
  962.1 12.2 convolution_convert_fusion.1
  975.0 10.9 convolution_convert_fusion.2
  1008.1 13.6 add_convert_fusion.4
  1021.7 6.4 all-to-all-done.1
  1029.5 22.4 %convolution_convert_fusion = bf16[8192,768]{1,0:T(8,128)(2,1)} fusion(bf16[1024,8192]{1,0:T(8,128)(2,1)} %reshape.527, bf16[1024,768]{1,0:T(8,128)(2,1)S(1)} %bitcast.319), kind=kOutput, calls=%fused_computation.67 | convolution fusion | flops 12891193344 | bytes 30932992 | tf_op jit(solution)/shard_map/tf,td->fd/dot_general | solution.py:87
  1053.4 61.4 %convolution_bitcast_fusion = f32[16,32,4,16,16,16]{1,4,5,3,2,0:T(8,128)} fusion(bf16[16,4,16,768,1,1]{3,2,5,4,1,0:T(8,128)(2,1)S(1)} %bitcast.320, bf16[32,16,16,768,1,1]{3,2,1,0,5,4:T(8,128)(2,1)} %bitcast.334), kind=kOutput, calls=%fused_computation.7 | convolution fusion | flops 12884901888 | bytes 47710208 | tf_op jit(solution)/shard_map/td,fd->tf/dot_general | solution.py:91
  1114.8 90.2 %copy.110 = f32[16,32,4,16,16,16]{1,5,4,3,2,0:T(8,128)} copy(f32[16,32,4,16,16,16]{1,4,5,3,2,0:T(8,128)} %convolution_bitcast_fusion) | data formatting | bytes 67108864 | tf_op jit(solution)/shard_map/transpose | solution.py:108
  1205.0 84.3 %copy.111 = f32[16,32,64,256]{3,1,2,0:T(8,128)} copy(f32[16,32,64,256]{1,3,2,0:T(8,128)} %bitcast.60) | data formatting | bytes 67108864 | tf_op jit(solution)/shard_map/reshape | solution.py:108
  1289.3 30.8 %convert_reduce_fusion = (f32[32]{0:T(128)S(1)}, bf16[16,32,64,256]{3,1,2,0:T(8,128)(2,1)}) fusion(f32[16,32,64,256]{3,1,2,0:T(8,128)} %copy.111, f32[16,64,256,32]{2,3,1,0:T(8,128)} %get-tuple-element.151, f32[32]{0:T(128)S(1)} %copy-done.85), kind=kLoop, calls=%fused_computation.22 | loop fusion | flops 192937952 | bytes 83886336 | tf_op jit(solution)/shard_map/reduce_sum | solution.py:287
  1325.6 29.0 %fusion.133 = f32[32,3,3,3]{0,3,2,1:T(4,128)S(1)} fusion(bf16[3,3,3,64,16,256]{5,3,2,1,0,4:T(8,128)(2,1)} %bitcast.328, bf16[16,32,64,256]{3,1,2,0:T(8,128)(2,1)} %get-tuple-element.126), kind=kOutput, calls=%fused_computation.177 | convolution fusion | flops 452984832 | bytes 30936448 | tf_op jit(solution)/shard_map/nohw,nkhw->ok/dot_general | solution.py:288
  1354.7 10.2 fusion.146
  1365.3 46.1 %all-reduce.2 = (f32[32,3,3,3]{0,3,2,1:T(4,128)}, f32[32]{0:T(128)}, f32[768]{0:T(1024)}, f32[768]{0:T(1024)}, f32[768]{0:T(1024)}, /*index=5*/f32[768]{0:T(1024...) all-reduce(f32[32,3,3,3]{0,3,2,1:T(4,128)S(1)} %fusion.133, ...), channel_id=1, replica_groups=mesh['items'=8,'rows'=4] {'items','rows'}, use_global_device_ids=true, to_apply=%region_15.16 | all-reduce | flops 10880 | bytes 87040 | tf_op jit(solution)/shard_map/psum | solution.py:293
  1413.2 27.3 %fusion.19 = bf16[16,32,66,258]{3,1,2,0:T(8,128)(2,1)} fusion(bf16[16,32,1,256]{3,1,2,0:T(8,128)(2,1)S(1)} %collective-permute-done.3, bf16[16,32,64,256]{3,1,2,0:T(8,128)(2,1)} %get-tuple-element.126, bf16[16,32,1,256]{3,1,2,0:T(8,128)(2,1)S(1)} %collective-permute-done.2), kind=kLoop, calls=%fused_computation.27 | loop fusion | flops 104620032 | bytes 34738176 | tf_op jit(solution)/shard_map/concatenate | solution.py:23
  1442.3 8.7 fusion.30
  1452.8 8.7 fusion.26
  1463.3 15.8 fusion.36
  1481.6 10.4 fusion.38
  1491.9 15.7 fusion.40
  1508.0 10.4 fusion.42
  1518.4 15.8 fusion.44
  1536.8 17.6 %add_bitcast_fusion = f32[16,3,64,256]{3,1,2,0:T(4,128)S(1)} fusion(f32[16,64,256,3]{2,3,1,0:T(4,128)} %fusion.30, f32[16,64,256,3]{2,3,1,0:T(4,128)} %fusion.36, f32[16,64,256,3]{2,3,1,0:T(4,128)} %fusion.38, f32[16,64,256,3]{2,3,1,0:T(4,128)} %fusion.146, f32[16,64,256,3]{2,3,1,0:T(4,128)} %fusion.40, f32[16,64,256,3]{2,3,1,0:T(4,128)} %fusion.42, ...), kind=kOutput, calls=%fused_computation.105 | convolution fusion | flops 56623104 | bytes 53477568 | tf_op jit(solution)/shard_map/nohw,oc->nchw/dot_general | solution.py:73
  1564.7 8.5 reduce-scatter.39.cloned.1.call-done
  1574.9 29.0 %reduce-scatter.43.cloned.1.call-done = bf16[192,1024]{1,0:T(8,128)(2,1)} async-done(((bf16[768,1024]{1,0:T(8,128)(2,1)}), bf16[192,1024]{1,0:T(8,128)(2,1)}) %reduce-scatter.43.cloned.1.call-update) | async-done | bytes 393232
  (339 shorter events, 126.7 us)
Async XLA Ops:
  7.2 542.3 %copy-start = (bf16[768,768]{1,0:T(8,128)(2,1)S(1)}, bf16[768,768]{1,0:T(8,128)(2,1)}, u32[]{:S(2)}) copy-start(bf16[768,768]{1,0:T(8,128)(2,1)} %param.33) | copy-start | bytes 3538948
  8.5 6.3 collective-permute-start
  10.8 5.2 collective-permute-start.1
  27.2 25.8 %copy-start.30 = (bf16[16,3,9,64,256]{4,3,2,1,0:T(8,128)(2,1)}, bf16[16,3,9,64,256]{4,3,2,1,0:T(8,128)(2,1)S(1)}, u32[]{:S(2)}) copy-start(bf16[16,3,9,64,256]{4,3,2,1,0:T(8,128)(2,1)S(1)} %fusion.99) | copy-start | bytes 42467332
  249.9 224.9 %copy-start.74 = (f32[768]{0:T(1024)S(1)}, f32[768]{0:T(1024)}, u32[]{:S(2)}) copy-start(f32[768]{0:T(1024)} %convert_element_type.268) | copy-start | bytes 9220
  474.8 24.8 %copy-start.75 = (bf16[768]{0:T(1024)(128)(2,1)S(1)}, bf16[768]{0:T(1024)(128)(2,1)}, u32[]{:S(2)}) copy-start(bf16[768]{0:T(1024)(128)(2,1)} %param.28) | copy-start | bytes 4612
  474.8 24.9 %copy-start.76 = (bf16[768]{0:T(1024)(128)(2,1)S(1)}, bf16[768]{0:T(1024)(128)(2,1)}, u32[]{:S(2)}) copy-start(bf16[768]{0:T(1024)(128)(2,1)} %param.37) | copy-start | bytes 4612
  474.8 25.5 %copy-start.77 = (bf16[768]{0:T(1024)(128)(2,1)S(1)}, bf16[768]{0:T(1024)(128)(2,1)}, u32[]{:S(2)}) copy-start(bf16[768]{0:T(1024)(128)(2,1)} %param.29) | copy-start | bytes 4612
  474.8 25.5 %copy-start.78 = (bf16[768]{0:T(1024)(128)(2,1)S(1)}, bf16[768]{0:T(1024)(128)(2,1)}, u32[]{:S(2)}) copy-start(bf16[768]{0:T(1024)(128)(2,1)} %param.38) | copy-start | bytes 4612
  474.8 26.1 %copy-start.79 = (bf16[768]{0:T(1024)(128)(2,1)S(1)}, bf16[768]{0:T(1024)(128)(2,1)}, u32[]{:S(2)}) copy-start(bf16[768]{0:T(1024)(128)(2,1)} %param.31) | copy-start | bytes 4612
  474.8 26.0 %copy-start.80 = (bf16[768]{0:T(1024)(128)(2,1)S(1)}, bf16[768]{0:T(1024)(128)(2,1)}, u32[]{:S(2)}) copy-start(bf16[768]{0:T(1024)(128)(2,1)} %param.34) | copy-start | bytes 4612
  474.8 26.0 %copy-start.81 = (bf16[768]{0:T(1024)(128)(2,1)S(1)}, bf16[768]{0:T(1024)(128)(2,1)}, u32[]{:S(2)}) copy-start(bf16[768]{0:T(1024)(128)(2,1)} %param.36) | copy-start | bytes 4612
  474.9 26.1 %copy-start.62 = (bf16[3072]{0:T(1024)(128)(2,1)S(1)}, bf16[3072]{0:T(1024)(128)(2,1)}, u32[]{:S(2)}) copy-start(bf16[3072]{0:T(1024)(128)(2,1)} %param.40) | copy-start | bytes 18436
  474.9 26.7 %copy-start.90 = (s32[16]{0:T(128)S(1)}, s32[16]{0:T(128)}, u32[]{:S(2)}) copy-start(s32[16]{0:T(128)} %param.23) | copy-start | bytes 196
  494.8 25.0 %all-to-all-start = ((bf16[16,4,16,768]{3,2,1,0:T(8,128)(2,1)}), bf16[16,4,16,768]{3,2,1,0:T(8,128)(2,1)S(1)}, u32[]{:S(2)}, u32[]{:S(2)}) async-start(bf16[16,4,16,768]{3,2,1,0:T(8,128)(2,1)} %bitcast.313), calls=%async_computation | async-start | bytes 3145728 | tf_op jit(solution)/shard_map/all_to_all | solution.py:165
  499.6 911.8 %reduce-scatter.35.cloned.1.call-start = ((), (), s32[]{:S(2)}) async-start(), calls=%async_computation.20 | async-start | bytes 1327104 | tf_op jit(solution)/shard_map/reduce_scatter | solution.py:323
  499.6 24.1 %copy-start.32 = (f32[768]{0:T(1024)}, f32[768]{0:T(1024)S(1)}, u32[]{:S(2)}) copy-start(f32[768]{0:T(1024)S(1)} %convert_element_type.275) | copy-start | bytes 9220
  500.3 23.5 %copy-start.42 = (f32[768]{0:T(1024)}, f32[768]{0:T(1024)S(1)}, u32[]{:S(2)}) copy-start(f32[768]{0:T(1024)S(1)} %convert_element_type.276) | copy-start | bytes 9220
  550.9 77.4 %copy-start.11 = (bf16[1024,768]{0,1:T(8,128)(2,1)}, bf16[1024,768]{0,1:T(8,128)(2,1)S(1)}, u32[]{:S(2)}) copy-start(bf16[1024,768]{0,1:T(8,128)(2,1)S(1)} %add_convert_fusion.7) | copy-start | bytes 4718596
  584.8 105.2 %copy-start.91 = (f32[12,512]{1,0:T(8,128)}, f32[12,512]{1,0:T(8,128)S(1)}, u32[]{:S(2)}) copy-start(f32[12,512]{1,0:T(8,128)S(1)} %get-tuple-element.152) | copy-start | bytes 73732
  618.0 82.8 %copy-start.92 = (f32[12,512]{1,0:T(8,128)}, f32[12,512]{1,0:T(8,128)S(1)}, u32[]{:S(2)}) copy-start(f32[12,512]{1,0:T(8,128)S(1)} %get-tuple-element.154) | copy-start | bytes 73732
  640.9 37.3 %copy-start.14 = (f32[1024,768]{1,0:T(8,128)}, f32[1024,768]{1,0:T(8,128)S(1)}, u32[]{:S(2)}) copy-start(f32[1024,768]{1,0:T(8,128)S(1)} %get-tuple-element.157) | copy-start | bytes 9437188
  640.9 37.3 %copy-start.44 = (f32[1024]{0:T(1024)}, f32[1024]{0:T(1024)S(1)}, u32[]{:S(2)}) copy-start(f32[1024]{0:T(1024)S(1)} %broadcast_multiply_fusion.1) | copy-start | bytes 12292
  641.5 36.7 %copy-start.52 = (f32[1024]{0:T(1024)}, f32[1024]{0:T(1024)S(1)}, u32[]{:S(2)}) copy-start(f32[1024]{0:T(1024)S(1)} %fusion.143) | copy-start | bytes 12292
  641.5 28.2 %slice-start = ((s8[4718592]{0:T(1024)(128)(4,1)}), s8[524288]{0:T(1024)(128)(4,1)S(1)}, s32[]{:S(2)}) async-start(s8[4718592]{0:T(1024)(128)(4,1)} %bitcast.335), calls=%async_computation.30 | async-start | bytes 1048576
  652.7 17.0 %slice-start.1 = ((s8[4718592]{0:T(1024)(128)(4,1)}), s8[4194304]{0:T(1024)(128)(4,1)S(1)}, s32[]{:S(2)}) async-start(s8[4718592]{0:T(1024)(128)(4,1)} %bitcast.335), calls=%async_computation.31 | async-start | bytes 8388608
  689.9 750.6 %reduce-scatter.33.cloned.1.call-start = ((), (), s32[]{:S(2)}) async-start(), calls=%async_computation.19 | async-start | bytes 1327104 | tf_op jit(solution)/shard_map/reduce_scatter | solution.py:320
  715.7 735.3 %reduce-scatter.29.cloned.1.call-start = ((), (), s32[]{:S(2)}) async-start(), calls=%async_computation.17 | async-start | bytes 1327104 | tf_op jit(solution)/shard_map/reduce_scatter | solution.py:314
  854.4 607.2 %reduce-scatter.31.cloned.1.call-start = ((), (), s32[]{:S(2)}) async-start(), calls=%async_computation.18 | async-start | bytes 1327104 | tf_op jit(solution)/shard_map/reduce_scatter | solution.py:317
  962.0 517.1 %reduce-scatter.41.cloned.1.call-start = ((), (), s32[]{:S(2)}) async-start(), calls=%async_computation.23 | async-start | bytes 5308416 | tf_op jit(solution)/shard_map/reduce_scatter | solution.py:329
  974.3 533.3 %reduce-scatter.37.cloned.1.call-start = ((), (), s32[]{:S(2)}) async-start(), calls=%async_computation.21 | async-start | bytes 5308416 | tf_op jit(solution)/shard_map/reduce_scatter | solution.py:326
  1004.5 23.6 %all-to-all-start.1 = ((bf16[4,16,16,768]{3,2,0,1:T(8,128)(2,1)}), bf16[4,16,16,768]{3,2,0,1:T(8,128)(2,1)S(1)}, u32[]{:S(2)}, u32[]{:S(2)}) async-start(bf16[4,16,16,768]{3,2,0,1:T(8,128)(2,1)} %copy.107), calls=%async_computation.1 | async-start | bytes 3145728 | tf_op jit(solution)/shard_map/all_to_all | solution.py:274
  1008.0 526.2 %reduce-scatter.27.cloned.1.call-start = ((), (), s32[]{:S(2)}) async-start(), calls=%async_computation.16 | async-start | bytes 14155776 | tf_op jit(solution)/shard_map/reduce_scatter | solution.py:311
  1028.1 23.9 %copy-start.12 = (bf16[4,16,16,768]{3,2,0,1:T(8,128)(2,1)}, bf16[4,16,16,768]{3,2,0,1:T(8,128)(2,1)S(1)}, u32[]{:S(2)}) copy-start(bf16[4,16,16,768]{3,2,0,1:T(8,128)(2,1)S(1)} %all-to-all-done.1) | copy-start | bytes 4718596
  1052.0 504.7 %reduce-scatter.51.cloned.1.call-start = ((), (), s32[]{:S(2)}) async-start(), calls=%async_computation.28 | async-start | bytes 245760
  1205.0 84.3 %copy-start.85 = (f32[32]{0:T(128)S(1)}, f32[32]{0:T(128)}, u32[]{:S(2)}) copy-start(f32[32]{0:T(128)} %copy-done.84) | copy-start | bytes 388
  1321.2 92.0 %collective-permute-start.3 = (bf16[16,32,1,256]{3,1,2,0:T(8,128)(2,1)S(1)}, bf16[16,32,1,256]{3,1,2,0:T(8,128)(2,1)S(1)}, u32[]{:S(2)}, u32[]{:S(2)}) collective-permute-start(bf16[16,32,1,256]{3,1,2,0:T(8,128)(2,1)S(1)} %get-tuple-element.131), channel_id=1, source_target_pairs={{1,0},{2,1},{3,2},{5,4},{6,5},{7,6},{9,8},{10,9},{11,10},{13,12},{... | collective-permute-start | bytes 786440 | tf_op jit(solution)/shard_map/ppermute | solution.py:27
  1322.5 90.7 %collective-permute-start.2 = (bf16[16,32,1,256]{3,1,2,0:T(8,128)(2,1)S(1)}, bf16[16,32,1,256]{3,1,2,0:T(8,128)(2,1)S(1)}, u32[]{:S(2)}, u32[]{:S(2)}) collective-permute-start(bf16[16,32,1,256]{3,1,2,0:T(8,128)(2,1)S(1)} %get-tuple-element.132), channel_id=1, source_target_pairs={{0,1},{1,2},{2,3},{4,5},{5,6},{6,7},{8,9},{9,10},{10,11},{12,13},{... | collective-permute-start | bytes 786440 | tf_op jit(solution)/shard_map/ppermute | solution.py:25
  1325.6 29.0 %copy-start.66 = (bf16[32,3,1,1]{0,3,2,1:T(2,128)(2,1)S(1)}, bf16[32,3,1,1]{0,3,2,1:T(2,128)(2,1)}, u32[]{:S(2)}) copy-start(bf16[32,3,1,1]{0,3,2,1:T(2,128)(2,1)} %get-tuple-element.144) | copy-start | bytes 580
  1413.1 29.1 %copy-start.83 = (bf16[32,3,1,1]{0,3,2,1:T(2,128)(2,1)S(1)}, bf16[32,3,1,1]{0,3,2,1:T(2,128)(2,1)}, u32[]{:S(2)}) copy-start(bf16[32,3,1,1]{0,3,2,1:T(2,128)(2,1)} %get-tuple-element.149) | copy-start | bytes 580
  1413.1 145.1 %reduce-scatter.49.cloned.1.call-start = ((), (), s32[]{:S(2)}) async-start(), calls=%async_computation.27 | async-start | bytes 245760
  1442.2 117.5 %reduce-scatter.45.cloned.1.call-start = ((), (), s32[]{:S(2)}) async-start(), calls=%async_computation.25 | async-start | bytes 245760
  1452.8 108.5 %reduce-scatter.47.cloned.1.call-start = ((), (), s32[]{:S(2)}) async-start(), calls=%async_computation.26 | async-start | bytes 245760
  1463.3 99.6 %reduce-scatter.53.cloned.1.call-start = ((), (), s32[]{:S(2)}) async-start(), calls=%async_computation.29 | async-start | bytes 737280
  1463.3 18.2 %copy-start.65 = (bf16[32,3,1,1]{0,3,2,1:T(2,128)(2,1)S(1)}, bf16[32,3,1,1]{0,3,2,1:T(2,128)(2,1)}, u32[]{:S(2)}) copy-start(bf16[32,3,1,1]{0,3,2,1:T(2,128)(2,1)} %get-tuple-element.143) | copy-start | bytes 580
  1481.3 92.0 %reduce-scatter.39.cloned.1.call-start = ((), (), s32[]{:S(2)}) async-start(), calls=%async_computation.22 | async-start | bytes 737280 | tf_op jit(solution)/shard_map/reduce_scatter | solution.py:349
  1507.7 96.2 %reduce-scatter.43.cloned.1.call-start = ((), (), s32[]{:S(2)}) async-start(), calls=%async_computation.24 | async-start | bytes 1966080
  1536.8 69.3 %copy-start.1 = (bf16[768,768]{1,0:T(8,128)(2,1)S(1)}, bf16[768,768]{1,0:T(8,128)(2,1)}, u32[]{:S(2)}) copy-start(bf16[768,768]{1,0:T(8,128)(2,1)} %param.33) | copy-start | bytes 3538948
  (69 other events, 457.7 us)
Sparse Core Ops, SparseCore 0:
  690.0 64.3 reduce-scatter.34
  757.8 63.3 reduce-scatter.32
  854.5 64.5 reduce-scatter.28
  962.2 64.3 reduce-scatter.30
  1030.1 94.2 reduce-scatter.40
  1127.9 95.1 reduce-scatter.36
  1226.7 208.0 reduce-scatter.26
  1437.2 18.7 reduce-scatter.50
  1458.5 19.7 reduce-scatter.48
  1481.1 19.7 reduce-scatter.44
  1503.9 19.7 reduce-scatter.46
  1526.6 22.0 reduce-scatter.52
  1551.2 22.0 reduce-scatter.38
  1575.7 28.1 reduce-scatter.42
where the time goes:
time: 1630 us; the launch traced here: 1610 us
  matrix products  673 us (41%)
  local copies, waits for them, and re-layouts  654 us (40%)
  other arithmetic  154 us (9%)
  waiting for transfers between devices  52.5 us (3%)
  blocking collectives  46.1 us (3%)
  starting transfers between devices  17.4 us (1%)
    reshape x1, local copies, waits for them, and re-layouts, to_patches(): tiles.transpose(0, 2, 4, 1, 3, 5)  225 us
    transpose x1, local copies, waits for them, and re-layouts, to_patches(): tiles.transpose(0, 2, 4, 1, 3, 5)  143 us
    dot_general x9, matrix products, convolve_back(): jnp.einsum('nohw,oc->nchw', window, kernel[:, :, row_tap, col_tap], prefe...  113 us
    dot_general x2, matrix products, on_device(): jnp.einsum('shqk,skhd->sqhd', score_grad, key_heads, preferred_element_ty...  105 us
    dot_general x2, matrix products, on_device(): jnp.einsum('shqk,sqhd->skhd', score_grad, query_part, preferred_element_t...  103 us
    dot_general x7, matrix products, inner_right(): jnp.einsum('td,fd->tf', left, right, preferred_element_type=jnp.float32)  98.3 us
    transpose x1, local copies, waits for them, and re-layouts, from_patches(): tiles.transpose(0, 3, 1, 4, 2, 5).reshape(count, chans, height, width)  90.2 us
    reshape x1, local copies, waits for them, and re-layouts, from_patches(): tiles.transpose(0, 3, 1, 4, 2, 5).reshape(count, chans, height, width)  84.3 us
  transfers between devices with their start and end apart: 20, of which 5 were waited for; matrix products, arithmetic and copies ran while one was open for 51% of the time, Pallas kernels for 0%

commit v1 on v0

v1 whole, which is shorter than its diff:
```python
import functools

import jax
import jax.numpy as jnp
from jax import lax
from jax.experimental import pallas as pl
from jax.experimental.pallas import tpu as pltpu
from jax.sharding import PartitionSpec as P

BF = jnp.bfloat16
F32 = jnp.float32
D = 768
HEADS = 12
HD = 64
FF = 3072
IMG = 256
PATCH = 16
CH = 32
CIN = 3
SEQ_ITEMS = 4
NPATCH = 256
TOK = 1024
NP = IMG // PATCH
PF = CH * PATCH * PATCH
HALF = 64
WIN = PATCH + 2
ONE_LANE = CIN * WIN
SLABS = (PATCH + 2) // 2
STEPS = PATCH // 2
FEAT = PF // STEPS
GELU_A = 0.7978845608028654
GELU_B = GELU_A * 0.044715
VMEM_CAP = 60 * 1024 * 1024


def mm(left, right):
    return jnp.dot(left, right, preferred_element_type=F32)


def mm_t(left, right):
    return lax.dot_general(left, right, (((1,), (1,)), ((), ())), preferred_element_type=F32)


def params(**extra):
    return pltpu.CompilerParams(vmem_limit_bytes=VMEM_CAP, **extra)


def whole(shape):
    zeros = (0,) * len(shape)
    return pl.BlockSpec(shape, lambda *_: zeros, pipeline_mode=pl.Buffered(1))


def gelu_pair(v):
    square = v * v
    gate = 0.5 + 0.5 * jnp.tanh(v * (GELU_A + GELU_B * square))
    act = v * gate
    slope = gate + act * (1.0 - gate) * (2.0 * GELU_A + (6.0 * GELU_B) * square)
    return act, slope


def patchify_kernel(img_ref, top_ref, bot_ref, x_ref, xt_ref, sel_ref, pix, rows):
    items, _, height, width = img_ref.shape
    nrow = height // PATCH
    group = items * nrow
    for ch in range(CIN):
        for item in range(items):
            full = img_ref[item, ch].astype(F32)
            for k in range(width // 128):
                pix[ch, k, item * height : (item + 1) * height, :] = full[:, k * 128 : (k + 1) * 128]
    patch_row = lax.broadcasted_iota(jnp.int32, (group, width), 0) % nrow
    for ch in range(CIN):
        cols = slice(ch * width, (ch + 1) * width)
        for r in range(PATCH):
            v = jnp.concatenate([pix[ch, k, pl.ds(r, group, stride=PATCH), :] for k in range(width // 128)], axis=1)
            rows[(r + 1) * group : (r + 2) * group, cols] = v.astype(BF)
            if r == PATCH - 1:
                up = jnp.where(patch_row == 0, top_ref[ch], pltpu.roll(v, 1, 0))
                rows[0:group, cols] = up.astype(BF)
            if r == 0:
                down = jnp.where(patch_row == nrow - 1, bot_ref[ch], pltpu.roll(v, group - 1, 0))
                rows[(PATCH + 1) * group : (PATCH + 2) * group, cols] = down.astype(BF)
    lane = lax.broadcasted_iota(jnp.int32, (1, NP * HALF), 1)
    col, spot = lane // HALF, lane % HALF
    for ch in range(CIN):
        inside = (spot >= WIN * ch) & (spot < WIN * (ch + 1))
        want = jnp.where(inside, PATCH * col + spot - WIN * ch - 1, -5)
        here = lax.broadcasted_iota(jnp.int32, (width, NP * HALF), 0)
        sel_ref[ch * width : (ch + 1) * width, :] = jnp.where(here == want, 1.0, 0.0).astype(BF)
    lane = lax.broadcasted_iota(jnp.int32, (group, 2 * HALF), 1)
    low = lane < HALF
    ones = (lane % HALF) == ONE_LANE
    for quarter in range(NP * HALF // 256):
        res = mm(rows[...], sel_ref[:, quarter * 256 : (quarter + 1) * 256])
        for j in range(SLABS):
            first = res[2 * j * group : (2 * j + 1) * group]
            second = res[(2 * j + 1) * group : (2 * j + 2) * group]
            for pair in range(2):
                a = first[:, pair * 128 : (pair + 1) * 128]
                b = second[:, pair * 128 : (pair + 1) * 128]
                even = jnp.where(ones, 1.0, jnp.where(low, a, pltpu.roll(b, HALF, 1)))
                odd = jnp.where(ones, 1.0, jnp.where(low, pltpu.roll(a, HALF, 1), b))
                at = (quarter * 4 + pair * 2) * group
                x_ref[j, at : at + group, :] = even.astype(BF)
                x_ref[j, at + group : at + 2 * group, :] = odd.astype(BF)
    for j in range(SLABS):
        xt_ref[j] = x_ref[j].T


def patchify(images, top, bot):
    items, _, height, width = images.shape
    tokens = items * (height // PATCH) * NP
    return pl.pallas_call(
        patchify_kernel,
        name="patchify",
        out_shape=(
            jax.ShapeDtypeStruct((SLABS, tokens, 128), BF),
            jax.ShapeDtypeStruct((SLABS, 128, tokens), BF),
            jax.ShapeDtypeStruct((CIN * width, NP * HALF), BF),
        ),
        scratch_shapes=[
            pltpu.VMEM((CIN, width // 128, items * height, 128), F32),
            pltpu.VMEM((WIN * tokens // NP, CIN * width), BF),
        ],
        compiler_params=params(),
    )(images, top, bot)


def stem_kernel(x_ref, t_ref, w_ref, pb_ref, tok_ref, act_ref, slope_ref, acc, nat):
    p = pl.program_id(0)
    tokens = acc.shape[0]
    group = tokens // NP

    @pl.when(p == 0)
    def _():
        acc[...] = jnp.broadcast_to(pb_ref[...], acc.shape)

    weight = w_ref[...].reshape(FEAT, D)
    for s in range(tokens // 256):
        rs = slice(s * 256, (s + 1) * 256)
        xs = jnp.concatenate([x_ref[p, rs, :], x_ref[p + 1, rs, :]], axis=1)
        for n in range(FEAT // 256):
            cs = slice(n * 256, (n + 1) * 256)
            pre = mm(xs, t_ref[:, cs])
            act, slope = gelu_pair(pre)
            act_ref[0, rs, cs] = act.astype(BF)
            slope_ref[0, rs, cs] = slope.astype(BF)
        acc[rs, :] += mm(act_ref[0, rs, :], weight)

    @pl.when(p == STEPS - 1)
    def _():
        for c in range(NP):
            for k in range(D // 128):
                nat[k, pl.ds(c, group, stride=NP), :] = acc[c * group : (c + 1) * group, k * 128 : (k + 1) * 128]
        for k in range(D // 128):
            tok_ref[:, k * 128 : (k + 1) * 128] = nat[k].astype(BF)


def stem_forward(x, taps, weight, bias):
    tokens = x.shape[1]
    return pl.pallas_call(
        stem_kernel,
        name="stem_forward",
        grid=(STEPS,),
        in_specs=[
            whole(x.shape),
            whole(taps.shape),
            pl.BlockSpec((CH, 1, 2 * PATCH, D), lambda p: (0, p, 0, 0)),
            whole((1, D)),
        ],
        out_specs=(
            whole((tokens, D)),
            pl.BlockSpec((1, tokens, FEAT), lambda p: (p, 0, 0)),
            pl.BlockSpec((1, tokens, FEAT), lambda p: (p, 0, 0)),
        ),
        out_shape=(
            jax.ShapeDtypeStruct((tokens, D), BF),
            jax.ShapeDtypeStruct((STEPS, tokens, FEAT), BF),
            jax.ShapeDtypeStruct((STEPS, tokens, FEAT), BF),
        ),
        scratch_shapes=[pltpu.VMEM((tokens, D), F32), pltpu.VMEM((D // 128, tokens, 128), F32)],
        compiler_params=params(),
    )(x, taps, weight, bias)


def norm_stats(v):
    centred = v - jnp.mean(v, axis=-1, keepdims=True)
    inv = lax.rsqrt(jnp.mean(centred * centred, axis=-1, keepdims=True) + 1e-06)
    return centred * inv, inv


def three_terms(v):
    hi = v.astype(BF)
    rest = v - hi.astype(F32)
    mid = rest.astype(BF)
    lo = (rest - mid.astype(F32)).astype(BF)
    return hi, mid, lo


def minus_terms(v, lane, base):
    hi, mid, lo = three_terms(-v)
    out = jnp.where(lane == 4, hi.astype(F32), base)
    out = jnp.where(lane == 5, mid.astype(F32), out)
    return jnp.where(lane == 6, lo.astype(F32), out).astype(BF)


def attend_kernel(tok_ref, g_ref, b_ref, qx_ref, kx_ref, wq_ref, wk_ref, wv_ref, qb_ref, vb_ref,
                  q_ref, k_ref, v_ref, o_ref, lx_ref, n1, kaug, vaug):
    @pl.when(pl.program_id(0) == 0)
    def _():
        for s in range(TOK // 128):
            rs = slice(s * 128, (s + 1) * 128)
            hat, _ = norm_stats(tok_ref[rs, :].astype(F32))
            n1[rs, :] = (hat * g_ref[...] + b_ref[...]).astype(BF)

    q_ref[...] = ((mm(n1[...], wq_ref[...]) + qb_ref[...]).astype(BF) * 0.125).astype(BF)
    k_ref[...] = mm(n1[...], wk_ref[...]).astype(BF)
    v_ref[...] = (mm(n1[...], wv_ref[...]) + vb_ref[...]).astype(BF)
    lane = lax.broadcasted_iota(jnp.int32, (NPATCH, 128), 1)
    low = lane < HD
    for i in range(SEQ_ITEMS):
        rs = slice(i * NPATCH, (i + 1) * NPATCH)
        kaug[rs, 128:256] = jnp.broadcast_to(kx_ref[i : i + 1, :], (NPATCH, 128)).astype(BF)
        vaug[rs, 128:256] = jnp.ones((NPATCH, 128), BF)
    for pair in range(2):
        cs = slice(pair * 128, (pair + 1) * 128)
        kaug[:, 0:128] = k_ref[:, cs]
        vaug[:, 0:128] = v_ref[:, cs]
        for i in range(SEQ_ITEMS):
            rs = slice(i * NPATCH, (i + 1) * NPATCH)
            span = slice(0, (i + 1) * NPATCH)
            qp = q_ref[rs, cs]
            qx = jnp.broadcast_to(qx_ref[i : i + 1, :], (NPATCH, 128))
            halves = []
            for h in range(2):
                mine = low if h == 0 else ~low
                qaug = jnp.concatenate([jnp.where(mine, qp, jnp.zeros_like(qp)), qx.astype(BF)], axis=1)
                scores = mm_t(qaug, kaug[span, :])
                top = jnp.max(scores, axis=1, keepdims=True)
                raised = jnp.exp(scores - top).astype(BF)
                out = mm(raised, vaug[span, :])
                total = out[:, 128:256]
                halves.append(out[:, 0:128] / total)
                lx_ref[pair * 2 + h, rs, :] = minus_terms(top + jnp.log(total), lane, qx)
            o_ref[rs, cs] = jnp.where(low, halves[0], halves[1]).astype(BF)


def attend(tokens, gain, shift, qx, kx, wq, wk, wv, qb, vb):
    col = pl.BlockSpec((D, 256), lambda g: (0, g))
    row = pl.BlockSpec((1, 256), lambda g: (0, g))
    out = pl.BlockSpec((TOK, 256), lambda g: (0, g))
    return pl.pallas_call(
        attend_kernel,
        name="attend",
        grid=(D // 256,),
        in_specs=[whole((TOK, D)), whole((1, D)), whole((1, D)), whole(qx.shape), whole(kx.shape),
                  col, col, col, row, row],
        out_specs=(out, out, out, out, pl.BlockSpec((4, TOK, 128), lambda g: (g, 0, 0))),
        out_shape=(jax.ShapeDtypeStruct((TOK, D), BF),) * 4 + (jax.ShapeDtypeStruct((HEADS, TOK, 128), BF),),
        scratch_shapes=[pltpu.VMEM((TOK, D), BF), pltpu.VMEM((TOK, 256), BF), pltpu.VMEM((TOK, 256), BF)],
        compiler_params=params(),
    )(tokens, gain, shift, qx, kx, wq, wk, wv, qb, vb)


def norm_back(e, hat, inv, gain):
    f = e * gain
    return inv * (f - jnp.mean(f, axis=-1, keepdims=True) - hat * jnp.mean(f * hat, axis=-1, keepdims=True))


def col_sum(v):
    return jnp.sum(v, axis=0, keepdims=True)


def store_square(ref, n, grad):
    items, rows, _, height, width = ref.shape
    for r in range(rows):
        ref[:, r, n] = grad[:, r * width : (r + 1) * width].reshape(items, height, width)


def mixer_kernel(tok_ref, att_ref, cot_ref, wo_ref, vec_ref, wh_ref, hb_ref, wr_ref,
                 out_ref, mid_ref, ag_ref, wog_ref, whg_ref, wrg_ref, sums_ref, hbg_ref,
                 middle, n2, n2t, cott, acc, back, act, hg):
    step = pl.program_id(0)
    last = pl.num_programs(0) - 1
    chunk = wh_ref.shape[1]
    blocks = [slice(s * 256, (s + 1) * 256) for s in range(TOK // 256)]

    @pl.when(step == 0)
    def _():
        for rs in blocks:
            row = tok_ref[rs, :].astype(F32) + mm(att_ref[rs, :], wo_ref[...]) + vec_ref[0:1, :]
            middle[rs, :] = row
            acc[rs, :] = row + vec_ref[3:4, :]
            back[rs, :] = jnp.zeros((256, D), F32)
            hat, _ = norm_stats(row)
            low = (hat * vec_ref[1:2, :] + vec_ref[2:3, :]).astype(BF)
            n2[rs, :] = low
            n2t[:, rs] = low.T
            cott[:, rs] = cot_ref[rs, :].T

    hsum = jnp.zeros((1, chunk), F32)
    for rs in blocks:
        for n in range(chunk // 128 // 3):
            cs = slice(n * 384, (n + 1) * 384)
            pre = mm(n2[rs, :], wh_ref[:, cs]) + hb_ref[:, cs]
            up = mm_t(cot_ref[rs, :], wr_ref[cs, :])
            a, slope = gelu_pair(pre)
            act[rs, cs] = a.astype(BF)
            hg[rs, cs] = (slope * up).astype(BF)
        acc[rs, :] += mm(act[rs, :], wr_ref[...])
        back[rs, :] += mm_t(hg[rs, :], wh_ref[...])
        hsum = hsum + col_sum(hg[rs, :].astype(F32))
    hbg_ref[...] = hsum
    grad = mm(n2t[...], hg[...]).astype(BF)
    whg_ref[...] = grad.reshape(whg_ref.shape)
    grad = mm(cott[...], act[...]).astype(BF)
    rows, width = wrg_ref.shape[1], wrg_ref.shape[3]
    for c in range(wrg_ref.shape[0]):
        wrg_ref[c] = grad[:, c * width : (c + 1) * width].reshape(rows, D // rows, width)

    @pl.when(step == last)
    def _():
        gsum = jnp.zeros((1, D), F32)
        bsum = jnp.zeros((1, D), F32)
        osum = jnp.zeros((1, D), F32)
        rsum = jnp.zeros((1, D), F32)
        for rs in blocks:
            out_ref[rs, :] = acc[rs, :].astype(BF)
            hat, inv = norm_stats(middle[rs, :])
            e = back[rs, :]
            gsum = gsum + col_sum(e * hat)
            bsum = bsum + col_sum(e)
            cot = cot_ref[rs, :].astype(F32)
            rsum = rsum + col_sum(cot)
            mid = cot + norm_back(e, hat, inv, vec_ref[1:2, :])
            mid_ref[rs, :] = mid
            low = mid.astype(BF)
            osum = osum + col_sum(low.astype(F32))
            n2[rs, :] = low
            n2t[:, rs] = att_ref[rs, :].T
            ag_ref[rs, :] = mm_t(low, wo_ref[...]).astype(BF)
        store_square(wog_ref, 0, mm(n2t[...], n2[...]).astype(BF))
        sums_ref[0:1, :] = gsum
        sums_ref[1:2, :] = bsum
        sums_ref[2:3, :] = osum
        sums_ref[3:4, :] = rsum


def mixer(tokens, attended, cotangent, wo, vecs, wh, hb, wr, items, rows):
    chunk = FF // rows
    per = items // rows
    return pl.pallas_call(
        mixer_kernel,
        name="mixer",
        grid=(rows,),
        in_specs=[
            whole((TOK, D)), whole((TOK, D)), whole((TOK, D)), whole((D, D)), whole(vecs.shape),
            pl.BlockSpec((D, chunk), lambda r: (0, r)),
            pl.BlockSpec((1, chunk), lambda r: (0, r)),
            pl.BlockSpec((chunk, D), lambda r: (r, 0)),
        ],
        out_specs=(
            whole((TOK, D)), whole((TOK, D)), whole((TOK, D)), whole((items, rows, 1, D // items, D // rows)),
            pl.BlockSpec((items, 1, D // items, chunk), lambda r: (0, r, 0, 0)),
            pl.BlockSpec((per, rows, D // rows, FF // items), lambda r: (r, 0, 0, 0)),
            whole((8, D)),
            pl.BlockSpec((1, chunk), lambda r: (0, r)),
        ),
        out_shape=(
            jax.ShapeDtypeStruct((TOK, D), BF),
            jax.ShapeDtypeStruct((TOK, D), F32),
            jax.ShapeDtypeStruct((TOK, D), BF),
            jax.ShapeDtypeStruct((items, rows, 1, D // items, D // rows), BF),
            jax.ShapeDtypeStruct((items, rows, D // items, chunk), BF),
            jax.ShapeDtypeStruct((items, rows, D // rows, FF // items), BF),
            jax.ShapeDtypeStruct((8, D), F32),
            jax.ShapeDtypeStruct((1, FF), F32),
        ),
        scratch_shapes=[
            pltpu.VMEM((TOK, D), F32), pltpu.VMEM((TOK, D), BF), pltpu.VMEM((D, TOK), BF),
            pltpu.VMEM((D, TOK), BF), pltpu.VMEM((TOK, D), F32), pltpu.VMEM((TOK, D), F32),
            pltpu.VMEM((TOK, chunk), BF), pltpu.VMEM((TOK, chunk), BF),
        ],
        compiler_params=params(),
    )(tokens, attended, cotangent, wo, vecs, wh, hb, wr)


def attend_back_kernel(tok_ref, g_ref, b_ref, kx_ref, mid_ref, q_ref, k_ref, v_ref, o_ref, ag_ref, lx_ref,
                       wq_ref, wk_ref, wv_ref,
                       tg_ref, sq_ref, sums_ref, qvs_ref,
                       n1t, back, kaug, vaug, qaug, oaug, dqt, dq, dk, dv, square):
    step = pl.program_id(0)
    blocks = [slice(s * 256, (s + 1) * 256) for s in range(TOK // 256)]

    @pl.when(step == 0)
    def _():
        for rs in blocks:
            hat, _ = norm_stats(tok_ref[rs, :].astype(F32))
            n1t[:, rs] = (hat * g_ref[...] + b_ref[...]).astype(BF).T
            back[rs, :] = jnp.zeros((256, D), F32)

    lane = lax.broadcasted_iota(jnp.int32, (NPATCH, 128), 1)
    low = lane < HD
    ones = jnp.where((lane >= 4) & (lane < 7), 1.0, 0.0).astype(BF)
    for i, rs in enumerate(blocks):
        kaug[rs, 128:256] = jnp.broadcast_to(kx_ref[i : i + 1, :], (NPATCH, 128)).astype(BF)
        vaug[rs, 128:256] = ones
    pick_row = lax.broadcasted_iota(jnp.int32, (256, 256), 0) % 128 // HD
    pick_col = lax.broadcasted_iota(jnp.int32, (256, 256), 1) // 128
    pick = jnp.where(pick_row == pick_col, 1.0, 0.0).astype(BF)
    for pair in range(2):
        cs = slice(pair * 128, (pair + 1) * 128)
        kaug[:, 0:128] = k_ref[:, cs]
        vaug[:, 0:128] = v_ref[:, cs]
        kt = k_ref[:, cs].T
        for rs in blocks:
            qp = q_ref[rs, cs]
            gp = ag_ref[rs, cs]
            prod = gp.astype(F32) * o_ref[rs, cs].astype(F32)
            hi = prod.astype(BF)
            both = jnp.concatenate([hi, (prod - hi.astype(F32)).astype(BF)], axis=1)
            dots = mm(both, pick)
            for h in range(2):
                mine = low if h == 0 else ~low
                qaug[h, rs, 0:128] = jnp.where(mine, qp, jnp.zeros_like(qp))
                qaug[h, rs, 128:256] = lx_ref[pair * 2 + h, rs, :]
                oaug[h, rs, 0:128] = jnp.where(mine, gp, jnp.zeros_like(gp))
                oaug[h, rs, 128:256] = minus_terms(dots[:, h * 128 : (h + 1) * 128], lane, jnp.zeros((NPATCH, 128), F32))
        for j, rs in enumerate(blocks):
            span = slice(j * NPATCH, TOK)
            parts_k, parts_v = [], []
            for h in range(2):
                probs = jnp.exp(mm_t(kaug[rs, :], qaug[h, span, :]))
                rise = mm_t(vaug[rs, :], oaug[h, span, :])
                grad = (probs * rise).astype(BF)
                probs_low = probs.astype(BF)
                parts_v.append(mm(probs_low, ag_ref[span, cs]))
                parts_k.append(mm(grad, q_ref[span, cs]))
                hs = slice(h * HD, (h + 1) * HD)
                part = mm(kt[hs, rs], grad)
                if j == 0:
                    dqt[hs, :] = part
                else:
                    dqt[hs, span] += part
            dk[rs, cs] = jnp.where(low, parts_k[0], parts_k[1]).astype(BF)
            dv[rs, cs] = jnp.where(low, parts_v[0], parts_v[1]).astype(BF)
        dq[:, cs] = (dqt[...].T * 0.125).astype(BF)
    qvs_ref[0:1, :] = col_sum(dq[...].astype(F32))
    qvs_ref[1:2, :] = col_sum(dv[...].astype(F32))
    for n, part in enumerate((dq, dk, dv)):
        square[n, step] = mm(n1t[...], part[...]).astype(BF)
    for rs in blocks:
        back[rs, :] += (
            mm_t(dq[rs, :], wq_ref[...]) + mm_t(dk[rs, :], wk_ref[...]) + mm_t(dv[rs, :], wv_ref[...])
        )

    @pl.when(step == pl.num_programs(0) - 1)
    def _():
        gsum = jnp.zeros((1, D), F32)
        bsum = jnp.zeros((1, D), F32)
        for rs in blocks:
            hat, inv = norm_stats(tok_ref[rs, :].astype(F32))
            e = back[rs, :]
            gsum = gsum + col_sum(e * hat)
            bsum = bsum + col_sum(e)
            tg_ref[rs, :] = (mid_ref[rs, :] + norm_back(e, hat, inv, g_ref[...])).astype(BF)
        sums_ref[0:1, :] = gsum
        sums_ref[1:2, :] = bsum
        for n in range(3):
            store_square(sq_ref, n, jnp.concatenate([square[n, g] for g in range(D // 256)], axis=1))


def attend_back(tokens, gain, shift, kx, mid, q, k, v, o, ag, lx, wq, wk, wv, items, rows):
    squares = (items, rows, 3, D // items, D // rows)
    col = pl.BlockSpec((D, 256), lambda g: (0, g))
    part = pl.BlockSpec((TOK, 256), lambda g: (0, g))
    return pl.pallas_call(
        attend_back_kernel,
        name="attend_back",
        grid=(D // 256,),
        in_specs=[whole((TOK, D)), whole((1, D)), whole((1, D)), whole(kx.shape), whole((TOK, D)),
                  part, part, part, part, part, pl.BlockSpec((4, TOK, 128), lambda g: (g, 0, 0)),
                  col, col, col],
        out_specs=(whole((TOK, D)), whole(squares), whole((8, D)), pl.BlockSpec((8, 256), lambda g: (0, g))),
        out_shape=(
            jax.ShapeDtypeStruct((TOK, D), BF),
            jax.ShapeDtypeStruct(squares, BF),
            jax.ShapeDtypeStruct((8, D), F32),
            jax.ShapeDtypeStruct((8, D), F32),
        ),
        scratch_shapes=[
            pltpu.VMEM((D, TOK), BF), pltpu.VMEM((TOK, D), F32),
            pltpu.VMEM((TOK, 256), BF), pltpu.VMEM((TOK, 256), BF),
            pltpu.VMEM((2, TOK, 256), BF), pltpu.VMEM((2, TOK, 256), BF),
            pltpu.VMEM((128, TOK), F32),
            pltpu.VMEM((TOK, 256), BF), pltpu.VMEM((TOK, 256), BF), pltpu.VMEM((TOK, 256), BF),
            pltpu.VMEM((3, D // 256, D, 256), BF),
        ],
        compiler_params=params(),
    )(tokens, gain, shift, kx, mid, q, k, v, o, ag, lx, wq, wk, wv)


def patch_grad_kernel(tg_ref, act_ref, tgc_ref, wg_ref, sums_ref, nat, tgt):
    tokens = nat.shape[1]
    group = tokens // NP

    @pl.when(pl.program_id(0) == 0)
    def _():
        for k in range(D // 128):
            nat[k] = tg_ref[:, k * 128 : (k + 1) * 128].astype(F32)
        total = jnp.zeros((1, D), F32)
        for c in range(NP):
            part = jnp.concatenate([nat[k, pl.ds(c, group, stride=NP), :] for k in range(D // 128)], axis=1)
            total = total + col_sum(part)
            tgc_ref[c * group : (c + 1) * group, :] = part.astype(BF)
        sums_ref[0:1, :] = total
        for s in range(tokens // 256):
            rs = slice(s * 256, (s + 1) * 256)
            tgt[:, rs] = tgc_ref[rs, :].T

    items, rows = wg_ref.shape[0], wg_ref.shape[1]
    width = FEAT // items
    for n in range(FEAT // 256):
        grad = mm(tgt[...], act_ref[0, :, n * 256 : (n + 1) * 256]).astype(BF)
        for c in range(256 // width):
            piece = grad[:, c * width : (c + 1) * width]
            wg_ref[n * (256 // width) + c, :, 0, :, :] = piece.reshape(rows, D // rows, width)


def patch_grad(tg, act, items, rows):
    tokens = tg.shape[0]
    return pl.pallas_call(
        patch_grad_kernel,
        name="patch_grad",
        grid=(STEPS,),
        in_specs=[whole((tokens, D)), pl.BlockSpec((1, tokens, FEAT), lambda p: (p, 0, 0))],
        out_specs=(
            whole((tokens, D)),
            pl.BlockSpec((items, rows, 1, D // rows, FEAT // items), lambda p: (0, 0, p, 0, 0)),
            whole((8, D)),
        ),
        out_shape=(
            jax.ShapeDtypeStruct((tokens, D), BF),
            jax.ShapeDtypeStruct((items, rows, STEPS, D // rows, FEAT // items), BF),
            jax.ShapeDtypeStruct((8, D), F32),
        ),
        scratch_shapes=[pltpu.VMEM((D // 128, tokens, 128), F32), pltpu.VMEM((D, tokens), BF)],
        compiler_params=params(),
    )(tg, act)


def stem_back_kernel(tg_ref, w_ref, slope_ref, xt_ref, t_ref, dx_ref, taps_ref, dxa, pg, cw_ref):
    p = pl.program_id(0)
    tokens = tg_ref.shape[0]
    weight = w_ref[...].reshape(FEAT, D)

    @pl.when(p == 0)
    def _():
        cw_ref[...] = jnp.zeros_like(cw_ref)
        dxa[0] = jnp.zeros((tokens, 128), F32)

    for s in range(tokens // 256):
        rs = slice(s * 256, (s + 1) * 256)
        for n in range(FEAT // 256):
            cs = slice(n * 256, (n + 1) * 256)
            da = mm_t(tg_ref[rs, :], weight[cs, :])
            pg[rs, cs] = (slope_ref[0, rs, cs].astype(F32) * da).astype(BF)
        back = mm_t(pg[rs, :], t_ref[...])
        dxa[p, rs, :] += back[:, 0:128]
        dxa[p + 1, rs, :] = back[:, 128:256]
    xt = jnp.concatenate([xt_ref[p], xt_ref[p + 1]], axis=0)
    cw_ref[...] += mm(xt, pg[...])

    @pl.when(p == STEPS - 1)
    def _():
        for j in range(SLABS):
            dx_ref[j] = dxa[j].astype(BF)
        taps_ref[...] = tap_grad_rows(cw_ref[...])


def stem_back(tg, weight, slope, xt, taps):
    tokens = tg.shape[0]
    return pl.pallas_call(
        stem_back_kernel,
        name="stem_back",
        grid=(STEPS,),
        in_specs=[
            whole((tokens, D)),
            pl.BlockSpec((CH, 1, 2 * PATCH, D), lambda p: (0, p, 0, 0)),
            pl.BlockSpec((1, tokens, FEAT), lambda p: (p, 0, 0)),
            whole(xt.shape),
            whole(taps.shape),
        ],
        out_specs=(whole((SLABS, tokens, 128)), whole((32, 128))),
        out_shape=(
            jax.ShapeDtypeStruct((SLABS, tokens, 128), BF),
            jax.ShapeDtypeStruct((32, 128), F32),
        ),
        scratch_shapes=[
            pltpu.VMEM((SLABS, tokens, 128), F32), pltpu.VMEM((tokens, FEAT), BF), pltpu.VMEM((256, FEAT), F32),
        ],
        compiler_params=params(),
    )(tg, weight, slope, xt, taps)


def image_grad_kernel(dx_ref, sel_ref, ig_ref, edge_ref, rows, flat):
    items, _, height, width = ig_ref.shape
    nrow = height // PATCH
    group = items * nrow
    low = lax.broadcasted_iota(jnp.int32, (group, 2 * HALF), 1) < HALF
    for j in range(SLABS):
        for pair in range(NP // 2):
            at = 2 * pair * group
            a = dx_ref[j, at : at + group, :].astype(F32)
            b = dx_ref[j, at + group : at + 2 * group, :].astype(F32)
            cs = slice(pair * 128, (pair + 1) * 128)
            rows[2 * j * group : (2 * j + 1) * group, cs] = jnp.where(low, a, pltpu.roll(b, HALF, 1)).astype(BF)
            rows[(2 * j + 1) * group : (2 * j + 2) * group, cs] = jnp.where(low, pltpu.roll(a, HALF, 1), b).astype(BF)
    patch_row = lax.broadcasted_iota(jnp.int32, (group, width), 0) % nrow
    for ch in range(CIN):
        cs = slice(ch * width, (ch + 1) * width)
        res = mm_t(rows[...], sel_ref[cs, :])
        head = res[0:group]
        tail = res[(PATCH + 1) * group : (PATCH + 2) * group]
        edge_ref[0, ch] = head
        edge_ref[1, ch] = tail
        for r in range(PATCH):
            v = res[(r + 1) * group : (r + 2) * group]
            if r == 0:
                v = v + jnp.where(patch_row == 0, 0.0, pltpu.roll(tail, 1, 0))
            if r == PATCH - 1:
                v = v + jnp.where(patch_row == nrow - 1, 0.0, pltpu.roll(head, group - 1, 0))
            flat[0, pl.ds(r, group, stride=PATCH), :] = v[:, 0:128]
            flat[1, pl.ds(r, group, stride=PATCH), :] = v[:, 128:256]
        for item in range(items):
            at = slice(item * height, (item + 1) * height)
            ig_ref[item, ch, :, 0:128] = flat[0, at, :]
            ig_ref[item, ch, :, 128:256] = flat[1, at, :]


def image_grad_call(dx, sel, items, height):
    group = items * height // PATCH
    return pl.pallas_call(
        image_grad_kernel,
        name="image_grad",
        out_shape=(
            jax.ShapeDtypeStruct((items, CIN, height, IMG), F32),
            jax.ShapeDtypeStruct((2, CIN, group, IMG), F32),
        ),
        scratch_shapes=[
            pltpu.VMEM((WIN * group, NP * HALF), BF),
            pltpu.VMEM((2, group * PATCH, 128), F32),
        ],
        compiler_params=params(),
    )(dx, sel)


def feature_parts(rows):
    feat = lax.broadcasted_iota(jnp.int32, (rows, FEAT), 1)
    return feat // (2 * PATCH), feat // PATCH % 2, feat % PATCH


def tap_rows(wide, ch, r, b, half):
    parts = []
    for r2 in range(2):
        a = r - r2
        parts.append(wide[9 * ch + 3 * a + b : 9 * ch + 3 * a + b + 1, :] if 0 <= a < 3 else jnp.zeros((1, FEAT), F32))
    return jnp.where(half == 0, parts[0], parts[1])


def tap_matrix_kernel(cw_ref, t_ref):
    chan, _, _ = feature_parts(32)
    expand = jnp.where(chan == lax.broadcasted_iota(jnp.int32, (32, FEAT), 0), 1.0, 0.0).astype(BF)
    wide = mm(cw_ref[...], expand)
    _, half, spot = feature_parts(1)
    line = lax.broadcasted_iota(jnp.int32, (HALF, FEAT), 0)
    for r in range(4):
        block = jnp.zeros((HALF, FEAT), F32)
        if r == 0:
            block = jnp.where(line == ONE_LANE, wide[27:28, :], block)
        for ch in range(CIN):
            for b in range(3):
                block = jnp.where(line == WIN * ch + b + spot, tap_rows(wide, ch, r, b, half), block)
        t_ref[r * HALF : (r + 1) * HALF, :] = block.astype(BF)


def tap_matrix(conv_weight, conv_bias):
    flat = jnp.concatenate([conv_weight.reshape(CH, 27), conv_bias[:, None], jnp.zeros((CH, 4), BF)], axis=1)
    return pl.pallas_call(
        tap_matrix_kernel,
        name="tap_matrix",
        out_shape=jax.ShapeDtypeStruct((4 * HALF, FEAT), BF),
        compiler_params=params(),
    )(flat.T)


def tap_grad_rows(full):
    chan, half, spot = feature_parts(1)
    line = lax.broadcasted_iota(jnp.int32, (HALF, FEAT), 0)
    sums = [[None] * 3 for _ in range(9)]
    for r in range(4):
        block = full[r * HALF : (r + 1) * HALF]
        for ch in range(CIN):
            for b in range(3):
                line_sum = jnp.sum(jnp.where(line == WIN * ch + b + spot, block, 0.0), axis=0, keepdims=True)
                for a in range(3):
                    if 0 <= r - a < 2:
                        part = jnp.where(half == r - a, line_sum, 0.0)
                        old = sums[3 * ch + b][a]
                        sums[3 * ch + b][a] = part if old is None else old + part
    lines = [sums[3 * ch + b][a] for ch in range(CIN) for a in range(3) for b in range(3)]
    lines.append(full[ONE_LANE : ONE_LANE + 1])
    lines.append(jnp.zeros((4, FEAT), F32))
    table = jnp.concatenate(lines, axis=0)
    chan, _, _ = feature_parts(128)
    expand = jnp.where(chan == lax.broadcasted_iota(jnp.int32, (128, FEAT), 0), 1.0, 0.0).astype(BF)
    hi, mid, lo = three_terms(table)
    return mm_t(hi, expand) + (mm_t(mid, expand) + mm_t(lo, expand))


def scatter_sum(chunks):
    shape = chunks.shape
    return lax.psum_scatter(
        chunks.reshape((shape[0] * shape[1],) + shape[2:]), ("items", "rows"), scatter_dimension=0, tiled=True
    )[0]


def unfold_kernel(in_ref, out_ref):
    width = in_ref.shape[2]
    for p in range(STEPS):
        turned = in_ref[p].astype(F32).T
        for c in range(width // (2 * PATCH)):
            at = c * PATCH * PATCH + p * 2 * PATCH
            out_ref[at : at + 2 * PATCH, :] = turned[c * 2 * PATCH : (c + 1) * 2 * PATCH, :]


def unfold(chunk):
    _, cols, width = chunk.shape
    return pl.pallas_call(
        unfold_kernel,
        name="unfold",
        out_shape=jax.ShapeDtypeStruct((STEPS * width, cols), F32),
        compiler_params=params(),
    )(chunk)


def on_device(
    images, item_segment, conv_weight, conv_bias, patch_weight, patch_bias, norm1_gain, norm1_bias,
    query_weight, query_bias, key_weight, value_weight, value_bias, output_weight, output_bias,
    norm2_gain, norm2_bias, hidden_weight, hidden_bias, result_weight, result_bias, cotangent,
):
    items, rows = lax.axis_size("items"), lax.axis_size("rows")
    count, _, height, _ = images.shape
    nrow = height // PATCH
    group = count * nrow

    def vec(v):
        return v.astype(F32).reshape(1, -1)

    down = [(i, i + 1) for i in range(rows - 1)]
    up = [(i + 1, i) for i in range(rows - 1)]
    top = lax.ppermute(images[:, :, height - 1], "rows", down)
    bot = lax.ppermute(images[:, :, 0], "rows", up)

    def spread(edge):
        edge = edge.transpose(1, 0, 2)[:, :, None, :].astype(F32)
        return jnp.broadcast_to(edge, (CIN, count, nrow, IMG)).reshape(CIN, group, IMG)

    segments = lax.dynamic_slice_in_dim(item_segment, lax.axis_index("rows") * SEQ_ITEMS, SEQ_ITEMS)
    lanes = jnp.arange(128)[None, :]
    same = lanes == segments[:, None]
    qx = jnp.where(same, 1.0, 0.0).astype(F32)
    kx = jnp.where((lanes < 4) & ~same, -1e30, 0.0) + jnp.where((lanes >= 4) & (lanes < 7), 1.0, 0.0)
    kx = kx.astype(F32)

    taps = tap_matrix(conv_weight, conv_bias)
    weight4 = patch_weight.reshape(CH, STEPS, 2 * PATCH, D)
    x, xt, sel = patchify(images, spread(top), spread(bot))
    embedded, act, slope = stem_forward(x, taps, weight4, vec(patch_bias))
    tokens = lax.all_to_all(
        embedded.reshape(count, nrow, NP, D), "rows", split_axis=0, concat_axis=1, tiled=True
    ).reshape(TOK, D)
    gain1, shift1 = vec(norm1_gain), vec(norm1_bias)
    q, k, v, attended, lx = attend(
        tokens, gain1, shift1, qx, kx, query_weight, key_weight, value_weight, vec(query_bias), vec(value_bias)
    )
    vecs = jnp.concatenate([vec(output_bias), vec(norm2_gain), vec(norm2_bias), vec(result_bias)], axis=0)
    block_out, middle_grad, attended_grad, wo_grad, wh_grad, wr_grad, sums2, hb_grad = mixer(
        tokens, attended, cotangent, output_weight, vecs, hidden_weight, vec(hidden_bias), result_weight, items, rows
    )
    wh_grad = scatter_sum(wh_grad)
    wr_grad = scatter_sum(wr_grad)
    wo_grad = scatter_sum(wo_grad)
    token_grad, squares, sums1, qvs = attend_back(
        tokens, gain1, shift1, kx, middle_grad, q, k, v, attended, attended_grad, lx,
        query_weight, key_weight, value_weight, items, rows,
    )
    squares = scatter_sum(squares)
    embed_grad = lax.all_to_all(
        token_grad.reshape(SEQ_ITEMS, NP, NP, D), "rows", split_axis=1, concat_axis=0, tiled=True
    ).reshape(-1, D)
    tgc, pw_grad, sums0 = patch_grad(embed_grad, act, items, rows)
    pw_grad = scatter_sum(pw_grad)
    dx, tap_grads = stem_back(tgc, weight4, slope, xt, taps)
    image_grad, edges = image_grad_call(dx, sel, count, height)
    edges = edges.reshape(2, CIN, count, nrow, IMG)
    from_below = lax.ppermute(edges[0, :, :, 0].astype(BF), "rows", up).astype(F32)
    from_above = lax.ppermute(edges[1, :, :, nrow - 1].astype(BF), "rows", down).astype(F32)
    image_grad = image_grad.at[:, :, height - 1].add(from_below.transpose(1, 0, 2))
    image_grad = image_grad.at[:, :, 0].add(from_above.transpose(1, 0, 2))
    small = lax.psum(
        (tap_grads[:, 0:CH], sums0[0:1], sums1[0:2], qvs[0:2], sums2[0:4], hb_grad), ("items", "rows")
    )
    return (
        block_out,
        image_grad,
        small[0][0:27].T.reshape(conv_weight.shape),
        small[0][27],
        unfold(pw_grad),
        small[1][0],
        small[2][0],
        small[2][1],
        squares[0].astype(F32),
        small[3][0],
        squares[1].astype(F32),
        squares[2].astype(F32),
        small[3][1],
        wo_grad[0].astype(F32),
        small[4][2],
        small[4][0],
        small[4][1],
        wh_grad.astype(F32),
        small[5][0],
        wr_grad.T.astype(F32),
        small[4][3],
    )


def solution(mesh):
    split = P("items", "rows")
    flat = P(("items", "rows"), None)
    image = P("items", None, "rows", None)
    return jax.shard_map(
        on_device,
        mesh=mesh,
        in_specs=(image, P("items")) + (P(),) * 19 + (flat,),
        out_specs=(
            flat, image, P(), P(), split, P(), P(), P(), split, P(), split, split,
            P(), split, P(), P(), P(), split, P(), split, P(),
        ),
        check_vma=False,
    )
```

time: 1630 us -> 777 us (0.48)
  matrix products: 673 us -> 0 us
  local copies, waits for them, and re-layouts: 654 us -> 22.6 us
  waiting for transfers between devices: 52.5 us -> 416 us
  Pallas kernels: 0 us -> 225 us
  other arithmetic: 154 us -> 12.7 us
  blocking collectives: 46.1 us -> 66.2 us
    dot_general x44 -> x0, matrix products: 673 us -> none  [the longest x9 113 us: convolve_back(): jnp.einsum('nohw,oc->nchw', window, kernel[:, :, row_tap, col_tap], prefe...]
    reduce_scatter x8 -> x5, waiting for transfers between devices: 8.56 us -> 399 us  [scatter_sum(): lax.psum_scatter(chunks.reshape((shape[0] * shape[1],) + shape[2:]), ('it...]
    reshape x4 -> x14, local copies, waits for them, and re-layouts: 311 us -> 6.58 us  [the longest x9 3.61 us: vec(): return v.astype(F32).reshape(1, -1)]
    transpose x2 -> x1, local copies, waits for them, and re-layouts: 233 us -> 0.01 us  [on_device(): small[0][0:27].T.reshape(conv_weight.shape)]
    pallas_call x0 -> x10, Pallas kernels: none -> 225 us  [the longest x1 49.4 us: mixer(): pl.pallas_call(mixer_kernel, name='mixer', grid=(rows,), in_specs=[whole(...]
    sub x3 -> x0, other arithmetic: 67.1 us -> none  [the longest x2 67.1 us: on_device(): raised = jnp.exp(scores - row_max)]
    convert_element_type x2 -> x0, local copies, waits for them, and re-layouts: 56.1 us -> none  [the longest x1 54 us: on_device(): activated = jax.nn.gelu(pre_act).astype(jnp.bfloat16)]
    reduce_sum x10 -> x0, other arithmetic: 39.9 us -> none  [the longest x1 30.8 us: on_device(): conv_bias_grad = jnp.sum(pre_grad.astype(jnp.float32), axis=(0, 2, 3))]
  transfers between devices with their start and end apart: 20 -> 10, of which waited for: 5 -> 5; matrix products, arithmetic and copies ran while one was open for 51% -> 4% of each run, Pallas kernels for 0% -> 14%
where the time goes in v1:
time: 777 us; the launch traced here: 769 us
  waiting for transfers between devices  416 us (54%)
  Pallas kernels  225 us (29%)
  blocking collectives  66.2 us (9%)
  local copies, waits for them, and re-layouts  22.6 us (3%)
  between operations  14.5 us (2%)
  starting transfers between devices  12.9 us (2%)
  other arithmetic  12.7 us (2%)
    reduce_scatter x5, waiting for transfers between devices, scatter_sum(): lax.psum_scatter(chunks.reshape((shape[0] * shape[1],) + shape[2:]), ('it...  399 us
    pallas_call x1, Pallas kernels, mixer(): pl.pallas_call(mixer_kernel, name='mixer', grid=(rows,), in_specs=[whole(...  49.4 us
    pallas_call x1, Pallas kernels, attend_back(): pl.pallas_call(attend_back_kernel, name='attend_back', grid=(D // 256,),...  44.9 us
    psum x1, blocking collectives, on_device(): lax.psum((tap_grads[:, 0:CH], sums0[0:1], sums1[0:2], qvs[0:2], sums2[0:4...  42.8 us
    pallas_call x1, Pallas kernels, stem_forward(): pl.pallas_call(stem_kernel, name='stem_forward', grid=(STEPS,), in_specs=...  34.2 us
    pallas_call x1, Pallas kernels, stem_back(): pl.pallas_call(stem_back_kernel, name='stem_back', grid=(STEPS,), in_spec...  31.4 us
    pallas_call x1, Pallas kernels, attend(): pl.pallas_call(attend_kernel, name='attend', grid=(D // 256,), in_specs=[...  24.9 us
    all_to_all x1, blocking collectives, on_device(): lax.all_to_all(token_grad.reshape(SEQ_ITEMS, NP, NP, D), 'rows', split_ax...  23.4 us
  transfers between devices with their start and end apart: 10, of which 5 were waited for; matrix products, arithmetic and copies ran while one was open for 4% of the time, Pallas kernels for 14%

profile of v1, /device:TPU:0, one launch (start us, length us, event | category | flops | bytes accessed | tf_op | source)
XLA Modules:
  0.0 769.2 jit_solution(1875417157371334476)
XLA Ops:
  7.2 1.1 fusion.6
  8.3 2.4 collective-permute-start
  10.7 1.3 collective-permute-start.1
  12.0 0.7 reshape.254
  12.8 1.3 maximum_bitcast_fusion.cw_ref
  14.1 1.3 reshape.286.pb_ref
  15.4 1.9 tap_matrix.1.t_ref
  17.4 0.7 reshape.253.bot_ref
  18.2 0.7 reshape.252.top_ref
  18.9 7.8 %patchify.1 = (bf16[9,1024,128]{2,1,0:T(8,128)(2,1)}, bf16[9,128,1024]{2,1,0:T(8,128)(2,1)}, bf16[768,1024]{1,0:T(8,128)(2,1)}) custom-call(bf16[16,3,64,256]{3,2,1,0:T(8,128)(2,1)} %img_ref.1, f32[3,64,256]{2,1,0:T(8,128)} %reshape.252.top_ref, f32[3,64,256]{2,1,0:T(8,128)} %reshape.253.bot_ref), custom_call_target="tpu_custom_call" | custom-call | tf_op jit(solution)/shard_map/patchify/pallas_call | solution.py:112
  26.7 34.2 %stem_forward.1 = (bf16[1024,768]{1,0:T(8,128)(2,1)}, bf16[8,1024,1024]{2,1,0:T(8,128)(2,1)}, bf16[8,1024,1024]{2,1,0:T(8,128)(2,1)}) custom-call(bf16[9,1024,128]{2,1,0:T(8,128)(2,1)} %get-tuple-element.75.x_ref, bf16[256,1024]{1,0:T(8,128)(2,1)} %tap_matrix.1.t_ref, bf16[32,8,32,768]{3,2,1,0:T(8,128)(2,1)} %bitcast.85, f32[1,768]{1,0:T(1,128)} %reshape.286.pb_ref), custom_call_target="tpu_custom_call" | custom-call | tf_op jit(solution)/shard_map/stem_forward/pallas_call | solution.py:160
  61.0 6.3 all-to-all-start
  70.6 0.6 maximum_convert_fusion.vec_ref
  71.2 0.7 select_add_fusion
  71.9 15.5 %all-to-all-done = bf16[16,4,16,768]{3,2,1,0:T(8,128)(2,1)S(1)} async-done(((bf16[16,4,16,768]{3,2,1,0:T(8,128)(2,1)}), bf16[16,4,16,768]{3,2,1,0:T(8,128)(2,1)S(1)}, u32[]{:S(2)}, u32[]{:S(2)}) %all-to-all-start) | async-done | bytes 1572896 | tf_op jit(solution)/shard_map/all_to_all | solution.py:779
  87.4 1.3 copy.61
  88.7 24.9 %attend.1 = (bf16[1024,768]{1,0:T(8,128)(2,1)}, bf16[1024,768]{1,0:T(8,128)(2,1)}, bf16[1024,768]{1,0:T(8,128)(2,1)}, bf16[1024,768]{1,0:T(8,128)(2,1)}, bf16[12,1024,128]{2,1,0:T(8,128)(2,1)}) custom-call(bf16[1024,768]{1,0:T(8,128)(2,1)} %bitcast.87, f32[1,768]{1,0:T(1,128)} %reshape.288.g_ref, f32[1,768]{1,0:T(1,128)} %reshape.290.b_ref, ...), custom_call_target="tpu_custom_call" | custom-call | tf_op jit(solution)/shard_map/attend/pallas_call | solution.py:251
  113.5 49.4 %mixer.1 = (bf16[1024,768]{1,0:T(8,128)(2,1)}, f32[1024,768]{1,0:T(8,128)}, bf16[1024,768]{1,0:T(8,128)(2,1)}, bf16[8,4,1,96,192]{4,3,2,1,0:T(8,128)(2,1)}, bf16...) custom-call(bf16[1024,768]{1,0:T(8,128)(2,1)} %bitcast.88, ...), custom_call_target="tpu_custom_call" | custom-call | tf_op jit(solution)/shard_map/mixer/pallas_call | solution.py:351
  163.0 44.9 %attend_back.1 = (bf16[1024,768]{1,0:T(8,128)(2,1)}, bf16[8,4,3,96,192]{4,3,2,1,0:T(8,128)(2,1)}, f32[8,768]{1,0:T(8,128)}, f32[8,768]{1,0:T(8,128)}) custom-call(bf16[1024,768]{1,0:T(8,128)(2,1)} %bitcast.89, f32[1,768]{1,0:T(1,128)} %reshape.288.g_ref, f32[1,768]{1,0:T(1,128)} %reshape.290.b_ref, f32[4,128]{1,0:T(4,128)} %get-tuple-element.189.kx_ref, ...), custom_call_target="tpu_custom_call" | custom-call | tf_op jit(solution)/shard_map/attend_back/pallas_call | solution.py:476
  208.0 0.7 reduce-scatter.14.cloned.1.call-update
  209.3 0.8 copy-done
  210.3 23.4 %all_to_all.30 = bf16[4,16,16,768]{3,2,0,1:T(8,128)(2,1)S(1)} all-to-all(bf16[4,16,16,768]{3,2,0,1:T(8,128)(2,1)S(1)} %copy.62), channel_id=1, replica_groups=mesh['items'=8,'rows'=4] {'rows'}, dimensions={1} | all-to-all | bytes 3145728 | tf_op jit(solution)/shard_map/all_to_all | solution.py:798
  233.7 1.3 copy.64
  235.0 20.5 %patch_grad.1 = (bf16[1024,768]{1,0:T(8,128)(2,1)}, bf16[8,4,8,192,128]{4,3,2,1,0:T(8,128)(2,1)}, f32[8,768]{1,0:T(8,128)}) custom-call(bf16[1024,768]{1,0:T(8,128)(2,1)} %bitcast.92, bf16[8,1024,1024]{2,1,0:T(8,128)(2,1)} %get-tuple-element.86.act_ref), custom_call_target="tpu_custom_call" | custom-call | tf_op jit(solution)/shard_map/patch_grad/pallas_call | solution.py:531
  255.5 0.7 slice.135
  256.2 0.7 slice.139
  256.9 31.4 %stem_back.1 = (bf16[9,1024,128]{2,1,0:T(8,128)(2,1)}, f32[32,128]{1,0:T(8,128)}) custom-call(bf16[1024,768]{1,0:T(8,128)(2,1)} %get-tuple-element.87.tg_ref, bf16[32,8,32,768]{3,2,1,0:T(8,128)(2,1)} %bitcast.86, bf16[8,1024,1024]{2,1,0:T(8,128)(2,1)} %get-tuple-element.88.slope_ref, bf16[9,128,1024]{2,1,0:T(8,128)(2,1)} %get-tuple-element.89.xt_ref, ...), custom_call_target="tpu_custom_call" | custom-call | tf_op jit(solution)/shard_map/stem_back/pallas_call | solution.py:582
  288.4 7.5 image_grad.1
  295.9 1.0 convert.35
  297.2 1.3 collective-permute-start.2
  298.5 0.8 slice_reduce_fusion.8
  299.2 42.8 %all-reduce = (f32[32,32]{1,0:T(8,128)S(1)}, f32[768]{0:T(1024)}, f32[2,768]{1,0:T(2,128)S(1)}, f32[2,768]{1,0:T(2,128)S(1)}, f32[4,768]{1,0:T(4,128)S(1)}, /*index=5*/f32[3072]{0:T(1024)}) all-reduce(f32[32,32]{1,0:T(8,128)S(1)} %bitcast.106, f32[768]{0:T(1024)S(1)} %slice_reduce_fusion.8, ...), channel_id=1, replica_groups=mesh['items'=8,'rows'=4] {'items','rows'}, use_global_device_ids=true, to_apply=%region_0.1 | all-reduce | flops 11008 | bytes 88064 | tf_op jit(solution)/shard_map/psum | solution.py:810
  342.0 0.6 slice_reduce_fusion
  344.4 1.3 collective-permute-start.3
  345.7 1.1 copy_add_fusion
  346.8 2.3 scatter-add.6
  349.1 1.1 slice_add_fusion
  350.2 2.3 scatter-add.9
  352.4 1.4 bitcast_convert_fusion.1
  353.9 18.5 %reduce-scatter.8.cloned.1.call-done = bf16[1,3,96,192]{3,2,1,0:T(8,128)(2,1)} async-done(((bf16[32,3,96,192]{3,2,1,0:T(8,128)(2,1)}), bf16[1,3,96,192]{3,2,1,0:T(8,128)(2,1)}) %reduce-scatter.8.cloned.1.call-update) | async-done | bytes 110608 | tf_op jit(solution)/shard_map/reduce_scatter | solution.py:722
  372.4 1.6 fusion
  373.9 111.0 %reduce-scatter.14.cloned.1.call-done = bf16[1,192,384]{2,1,0:T(8,128)(2,1)} async-done(((bf16[32,192,384]{2,1,0:T(8,128)(2,1)}), bf16[1,192,384]{2,1,0:T(8,128)(2,1)}) %reduce-scatter.14.cloned.1.call-update) | async-done | bytes 147472 | tf_op jit(solution)/shard_map/reduce_scatter | solution.py:722
  484.9 1.6 convert_bitcast_fusion
  486.5 109.8 %reduce-scatter.12.cloned.1.call-done = bf16[1,96,768]{2,1,0:T(8,128)(2,1)} async-done(((bf16[32,96,768]{2,1,0:T(8,128)(2,1)}), bf16[1,96,768]{2,1,0:T(8,128)(2,1)}) %reduce-scatter.12.cloned.1.call-update) | async-done | bytes 147472 | tf_op jit(solution)/shard_map/reduce_scatter | solution.py:722
  596.3 1.6 bitcast_convert_fusion
  598.0 159.8 %reduce-scatter.6.cloned.1.call-done = bf16[1,8,192,128]{3,2,1,0:T(8,128)(2,1)} async-done(((bf16[32,8,192,128]{3,2,1,0:T(8,128)(2,1)}), bf16[1,8,192,128]{3,2,1,0:T(8,128)(2,1)}) %reduce-scatter.6.cloned.1.call-update) | async-done | bytes 393232 | tf_op jit(solution)/shard_map/reduce_scatter | solution.py:722
  757.7 2.2 unfold.1
  759.9 2.4 copy.70
  (73 shorter events, 6.3 us)
Async XLA Ops:
  8.3 9.8 %collective-permute-start = (bf16[16,3,256]{2,0,1:T(8,128)(2,1)S(1)}, bf16[16,3,256]{2,0,1:T(8,128)(2,1)S(1)}, u32[]{:S(2)}, u32[]{:S(2)}) collective-permute-start(bf16[16,3,256]{2,0,1:T(8,128)(2,1)S(1)} %bitcast.103), channel_id=1, source_target_pairs={{0,1},{1,2},{2,3},{4,5},{5,6},{6,7},{8,9},{9,10},{10,11},{12,13},{... | collective-permute-start | bytes 73736 | tf_op jit(solution)/shard_map/ppermute | solution.py:761
  10.7 6.6 collective-permute-start.1
  60.9 6.6 copy-start.5
  60.9 7.2 copy-start.6
  60.9 7.8 %copy-start.7 = (bf16[768]{0:T(1024)(128)(2,1)S(1)}, bf16[768]{0:T(1024)(128)(2,1)}, u32[]{:S(2)}) copy-start(bf16[768]{0:T(1024)(128)(2,1)} %param.35) | copy-start | bytes 4612
  60.9 8.3 %copy-start.8 = (bf16[768]{0:T(1024)(128)(2,1)S(1)}, bf16[768]{0:T(1024)(128)(2,1)}, u32[]{:S(2)}) copy-start(bf16[768]{0:T(1024)(128)(2,1)} %param.38) | copy-start | bytes 4612
  60.9 8.9 %copy-start.9 = (bf16[768]{0:T(1024)(128)(2,1)S(1)}, bf16[768]{0:T(1024)(128)(2,1)}, u32[]{:S(2)}) copy-start(bf16[768]{0:T(1024)(128)(2,1)} %param.40) | copy-start | bytes 4612
  61.0 8.9 %copy-start.10 = (bf16[768]{0:T(1024)(128)(2,1)S(1)}, bf16[768]{0:T(1024)(128)(2,1)}, u32[]{:S(2)}) copy-start(bf16[768]{0:T(1024)(128)(2,1)} %param.41) | copy-start | bytes 4612
  61.0 8.9 %copy-start.11 = (bf16[768]{0:T(1024)(128)(2,1)S(1)}, bf16[768]{0:T(1024)(128)(2,1)}, u32[]{:S(2)}) copy-start(bf16[768]{0:T(1024)(128)(2,1)} %param.42) | copy-start | bytes 4612
  61.0 8.9 %copy-start.12 = (bf16[768]{0:T(1024)(128)(2,1)S(1)}, bf16[768]{0:T(1024)(128)(2,1)}, u32[]{:S(2)}) copy-start(bf16[768]{0:T(1024)(128)(2,1)} %param.46) | copy-start | bytes 4612
  61.0 8.9 %copy-start.4 = (bf16[3072]{0:T(1024)(128)(2,1)S(1)}, bf16[3072]{0:T(1024)(128)(2,1)}, u32[]{:S(2)}) copy-start(bf16[3072]{0:T(1024)(128)(2,1)} %param.44) | copy-start | bytes 18436
  61.0 9.5 %copy-start.13 = (s32[16]{0:T(128)S(1)}, s32[16]{0:T(128)}, u32[]{:S(2)}) copy-start(s32[16]{0:T(128)} %param.27) | copy-start | bytes 196
  61.0 26.3 %all-to-all-start = ((bf16[16,4,16,768]{3,2,1,0:T(8,128)(2,1)}), bf16[16,4,16,768]{3,2,1,0:T(8,128)(2,1)S(1)}, u32[]{:S(2)}, u32[]{:S(2)}) async-start(bf16[16,4,16,768]{3,2,1,0:T(8,128)(2,1)} %bitcast.98), calls=%async_computation | async-start | bytes 3145728 | tf_op jit(solution)/shard_map/all_to_all | solution.py:779
  67.3 285.1 %reduce-scatter.10.cloned.1.call-start = ((), (), s32[]{:S(2)}) async-start(), calls=%async_computation.9 | async-start | bytes 1622016 | tf_op jit(solution)/shard_map/reduce_scatter | solution.py:722
  163.0 209.4 %reduce-scatter.8.cloned.1.call-start = ((), (), s32[]{:S(2)}) async-start(), calls=%async_computation.8 | async-start | bytes 4866048 | tf_op jit(solution)/shard_map/reduce_scatter | solution.py:722
  207.9 276.9 %reduce-scatter.14.cloned.1.call-start = ((), (), s32[]{:S(2)}) async-start(), calls=%async_computation.11 | async-start | bytes 4866048 | tf_op jit(solution)/shard_map/reduce_scatter | solution.py:722
  208.7 387.7 %reduce-scatter.12.cloned.1.call-start = ((), (), s32[]{:S(2)}) async-start(), calls=%async_computation.10 | async-start | bytes 4866048 | tf_op jit(solution)/shard_map/reduce_scatter | solution.py:722
  208.7 1.4 copy-start
  209.2 548.5 %reduce-scatter.6.cloned.1.call-start = ((), (), s32[]{:S(2)}) async-start(), calls=%async_computation.7 | async-start | bytes 12976128 | tf_op jit(solution)/shard_map/reduce_scatter | solution.py:722
  255.4 1.5 copy-start.3
  288.4 10.8 %copy-start.1 = (f32[32,128]{1,0:T(8,128)S(1)}, f32[32,128]{1,0:T(8,128)}, u32[]{:S(2)}) copy-start(f32[32,128]{1,0:T(8,128)} %get-tuple-element.94) | copy-start | bytes 49156
  288.4 10.8 %copy-start.2 = (f32[1,3072]{1,0:T(1,128)S(1)}, f32[1,3072]{1,0:T(1,128)}, u32[]{:S(2)}) copy-start(f32[1,3072]{1,0:T(1,128)} %get-tuple-element.103) | copy-start | bytes 36868
  297.2 48.6 %collective-permute-start.2 = (bf16[3,16,256]{2,1,0:T(8,128)(2,1)S(1)}, bf16[3,16,256]{2,1,0:T(8,128)(2,1)S(1)}, u32[]{:S(2)}, u32[]{:S(2)}) collective-permute-start(bf16[3,16,256]{2,1,0:T(8,128)(2,1)S(1)} %bitcast.102), channel_id=1, source_target_pairs={{1,0},{2,1},{3,2},{5,4},{6,5},{7,6},{9,8},{10,9},{11,10},{13,12},{... | collective-permute-start | bytes 73736 | tf_op jit(solution)/shard_map/ppermute | solution.py:806
  344.4 4.7 collective-permute-start.3
Sparse Core Ops, SparseCore 0:
  163.1 97.3 reduce-scatter.9
  266.0 106.3 reduce-scatter.7
  378.7 106.0 reduce-scatter.13
  490.2 106.0 reduce-scatter.11
  603.2 154.4 reduce-scatter.5
